TPU v7x, 128 devices: a whole 4x4x4 slice. The times are simulated.
128 devices in a mesh: gx: 32 (over y, z, core), gy: 4 (over x).
Axes of the slice: x: 4, y: 4, z: 4, core: 2. Of those that a mesh axis runs over, the one named last changes fastest.
Arguments:
- velocity: float32 [3, 512, 64, 1024], P(None, 'gx', 'gy'), may hold values from -6 to 6
- cotangent: float32 [3, 512, 64, 1024], P(None, 'gx', 'gy'), may hold values from -6 to 6
- points: float32 [3, 18432], replicated, as said below
- motion: float32 [3, 18432], replicated, may hold values from -6 to 6
- coef: float32 [49152], P(('gx', 'gy')), may hold values from 0.5 to 4
- readers: int32 [96, 16], replicated, may hold values from 0 to 262143, as said below
- owner: int32 [96], replicated, may hold values from 0 to 127, as said below
Outputs:
- velocity_out: float32 [3, 512, 64, 1024], P(None, 'gx', 'gy')
- coef_grad: float32 [49152], P(('gx', 'gy'))
Inputs may be any that keep to these rules, and one draw needn't show every extreme that they name: `readers`: each rotor's 16 tiles form a 4 x 4 block of cells in the first two dimensions at one tile along the third, listed row by row, all on one device; no device holds tiles of more than 4 rotors, and some device holds tiles of exactly 4. `owner`: no device owns more than 2 rotors, and some device owns exactly 2. Each rotor's points lie inside its block of cells in the first two coordinates and inside its tile along the third.
All inputs are finite; a program needn't handle non-finite values.
Results may differ from a plain program's by a relative error of at most 0.0003.
Values sent between devices are 32-bit elements; how exact they have to be, the bound alone decides.
No kernel may reach another device: no remote copies, remote signals or barrier semaphores. Data moves between devices by JAX's collectives and lax.ppermute only.
A program may use at most 64 MiB of HBM per device.

v0:
```python
import math

import jax
import jax.numpy as jnp
from jax import lax
from jax.sharding import PartitionSpec as P

HOST_MAX = 4


gauss_norm = math.pi ** (-1.5)
time_step = 0.5
viscosity = 0.15


def extended(cells, sides, width):
    for axis, dim in sides:
        count = lax.axis_size(axis)
        ends = count - 1
        head = lax.slice_in_dim(cells, 0, width, axis=dim)
        tail = lax.slice_in_dim(cells, cells.shape[dim] - width, cells.shape[dim], axis=dim)
        cells = jnp.concatenate(
            [
                lax.ppermute(tail, axis, [(i, (i + 1) % count) for i in range(ends)]),
                cells,
                lax.ppermute(head, axis, [((i + 1) % count, i) for i in range(ends)]),
            ],
            axis=dim,
        )
    return cells


def cell_kernel(tile_ids, positions, full_y, tiles_z):
    tile_i = tile_ids // (full_y * tiles_z)
    tile_j = tile_ids // tiles_z % full_y
    tile_k = tile_ids % tiles_z
    within = jnp.arange(128, dtype=jnp.int32)
    coord_x = tile_i.astype(jnp.float32)[:, :, None, None]
    coord_y = tile_j.astype(jnp.float32)[:, :, None, None]
    coord_z = (tile_k[:, :, None] * 128 + within[None, None, :]).astype(jnp.float32)[:, :, :, None]
    delta_x = coord_x - positions[0][:, None, None, :]
    delta_y = coord_y - positions[1][:, None, None, :]
    delta_z = coord_z - positions[2][:, None, None, :]
    return gauss_norm * jnp.exp(-(delta_x * delta_x + delta_y * delta_y + delta_z * delta_z))


def laplace_term(padded, center):
    total = padded[:, 2:, 1:-1, 1:-1] + padded[:, :-2, 1:-1, 1:-1]
    total = total + padded[:, 1:-1, 2:, 1:-1] + padded[:, 1:-1, :-2, 1:-1]
    total = total + padded[:, 1:-1, 1:-1, 2:] + padded[:, 1:-1, 1:-1, :-2]
    return total - 6.0 * center


def owner_slots(owner, own_max):
    index = jnp.arange(owner.shape[0], dtype=jnp.int32)
    same = owner[:, None] == owner[None, :]
    earlier = index[None, :] < index[:, None]
    rank_owner = jnp.sum((same & earlier).astype(jnp.int32), axis=1)
    return (owner * own_max + rank_owner, rank_owner)


def per_device(velocity, cotangent, points, motion, coef, readers, owner):
    cx_n, cy_n, cz_n = (velocity.shape[1], velocity.shape[2], velocity.shape[3])
    tiles_z = cz_n // 128
    n_gy = lax.axis_size("gy")
    full_y = cy_n * n_gy
    rotors = readers.shape[0]
    points_n = points.shape[1] // rotors
    own_max = coef.shape[0] // points_n
    device_id = lax.axis_index("gx") * n_gy + lax.axis_index("gy")
    rotor_index = jnp.arange(rotors, dtype=jnp.int32)
    first_tile = readers[:, 0]
    first_i = first_tile // (full_y * tiles_z)
    first_j = first_tile // tiles_z % full_y
    host_dev = first_i // cx_n * n_gy + first_j // cy_n
    mine = host_dev == device_id
    rank_mine = jnp.cumsum(mine.astype(jnp.int32)) - 1
    hosted_pick = mine[None, :] & (
        rank_mine[None, :] == jnp.arange(HOST_MAX, dtype=jnp.int32)[:, None]
    )
    is_live = jnp.any(hosted_pick, axis=1)
    hosted = jnp.sum(jnp.where(hosted_pick, rotor_index[None, :], 0), axis=1)
    tile_ids = readers[hosted]
    tile_i = tile_ids // (full_y * tiles_z)
    tile_j = tile_ids // tiles_z % full_y
    local_tiles = (tile_i % cx_n * cy_n + tile_j % cy_n) * tiles_z + tile_ids % tiles_z
    flat_local = local_tiles.reshape(-1)
    positions = points.reshape(3, rotors, points_n)[:, hosted]
    kernel = (
        cell_kernel(tile_ids, positions, full_y, tiles_z)
        * is_live.astype(jnp.float32)[:, None, None, None]
    )
    pick_float = hosted_pick.astype(jnp.float32)
    slot_ids, rank_owner = owner_slots(owner, own_max)
    owned_pick = (
        (owner[None, :] == device_id)
        & (rank_owner[None, :] == jnp.arange(own_max, dtype=jnp.int32)[:, None])
    ).astype(jnp.float32)
    hosted_slots = slot_ids[hosted]
    motion_rot = motion.reshape(3, rotors, points_n)

    def local_sample(field_in):
        gathered = field_in.reshape(3, cx_n * cy_n * tiles_z, 128)[:, local_tiles]
        return jnp.einsum("htcp,khtc->khp", kernel, gathered, precision=lax.Precision.HIGHEST)

    def sample(field_in):
        placed = jnp.einsum(
            "hr,khp->krp", pick_float, local_sample(field_in), precision=lax.Precision.HIGHEST
        )
        return placed.reshape(3, rotors * points_n)

    def hosted_force(shape_term):
        owned_term = jnp.einsum(
            "or,krp->kop", owned_pick, shape_term, precision=lax.Precision.HIGHEST
        )
        owned_force = coef.reshape(own_max, points_n)[None] * owned_term
        spread_out = lax.all_gather(
            owned_force.reshape(3, own_max * points_n), ("gx", "gy"), axis=1, tiled=True
        )
        return spread_out.reshape(3, -1, points_n)[:, hosted_slots]

    def substep(velocity_now):
        samples = lax.psum(sample(velocity_now), ("gx", "gy")).reshape(3, rotors, points_n)
        relative = samples - motion_rot
        speed = jnp.sqrt(jnp.sum(relative * relative, axis=0))
        shape_term = speed[None] * relative
        force_rows = hosted_force(shape_term)
        contrib = jnp.einsum("htcp,khp->khtc", kernel, force_rows, precision=lax.Precision.HIGHEST)
        forcing = jnp.zeros((3, cx_n * cy_n * tiles_z, 128), jnp.float32)
        forcing = (
            forcing.at[:, flat_local].add(contrib.reshape(3, -1, 128)).reshape(3, cx_n, cy_n, cz_n)
        )
        widened = extended(velocity_now, (("gx", 1), ("gy", 2)), 1)
        padded = jnp.pad(widened, ((0, 0), (0, 0), (0, 0), (1, 1)))
        return (
            velocity_now + time_step * (viscosity * laplace_term(padded, velocity_now) + forcing),
            shape_term,
        )

    velocity_mid, unused_term = substep(velocity)
    velocity_out, shape_second = substep(velocity_mid)
    sampled_adjoint = lax.psum(sample(cotangent), ("gx", "gy")).reshape(3, rotors, points_n)
    grad_rows = time_step * jnp.sum(sampled_adjoint * shape_second, axis=0)
    coef_grad = jnp.einsum("or,rp->op", owned_pick, grad_rows, precision=lax.Precision.HIGHEST)
    return (velocity_out, coef_grad.reshape(-1))


def solution(mesh):
    return jax.shard_map(
        per_device,
        mesh=mesh,
        in_specs=(
            P(None, "gx", "gy", None),
            P(None, "gx", "gy", None),
            P(),
            P(),
            P(("gx", "gy")),
            P(),
            P(),
        ),
        out_specs=(P(None, "gx", "gy", None), P(("gx", "gy"))),
        check_vma=False,
    )
```

profile of v0, /device:TPU:1, one launch (start us, length us, event | category | flops | bytes accessed | tf_op | source)
XLA Modules:
  0.0 596.2 jit_solution(978152103533315495)
XLA Ops:
  12.6 2.8 reshape.754
  15.5 10.0 %copy.38 = f32[3,2048,128]{2,0,1:T(4,128)} copy(f32[3,2048,128]{2,1,0:T(8,128)S(1)} %reshape.754) | data formatting | bytes 6291456 | tf_op jit(solution)/shard_map/reshape | solution.py:103
  25.5 2.8 gather_fusion.1
  28.5 6.0 %fusion.42 = f32[3,4,192]{2,0,1:T(4,128)S(1)} fusion(f32[3,4,16,128]{3,0,2,1:T(4,128)S(1)} %bitcast.120, f32[4]{0:T(128)S(1)} %broadcast_select_fusion, f32[4,192]{1,0:T(4,128)S(1)} %bitcast.128, f32[4,16,128]{2,1,0:T(8,128)S(1)} %add_convert_fusion, f32[4,16,192]{2,1,0:T(8,128)S(1)} %multiply_add_fusion), kind=kOutput, calls=%fused_computation.80 | convolution fusion | flops 64487424 | bytes 192528 | tf_op jit(solution)/shard_map/htcp,khtc->khp/dot_general | solution.py:104
  38.7 4.9 collective-permute-start.1
  50.3 4.5 reshape.767
  54.8 6.5 %copy.49 = f32[3,2048,128]{2,0,1:T(4,128)} copy(f32[3,2048,128]{2,1,0:T(8,128)} %reshape.767) | data formatting | bytes 6291456 | tf_op jit(solution)/shard_map/reshape | solution.py:103
  61.3 2.9 gather_fusion.7
  64.2 6.0 %fusion.44 = f32[3,4,192]{2,0,1:T(4,128)S(1)} fusion(f32[3,4,16,128]{3,0,2,1:T(4,128)S(1)} %bitcast.122, f32[4]{0:T(128)S(1)} %copy-done.32, f32[4,192]{1,0:T(4,128)S(1)} %bitcast.130, f32[4,16,128]{2,1,0:T(8,128)S(1)} %add_convert_fusion, f32[4,16,192]{2,1,0:T(8,128)S(1)} %multiply_add_fusion), kind=kOutput, calls=%fused_computation.82 | convolution fusion | flops 64487424 | bytes 192528 | tf_op jit(solution)/shard_map/htcp,khtc->khp/dot_general | solution.py:104
  73.5 109.5 %all-reduce.6.cloned.1.call-done = f32[3,18432]{1,0:T(4,128)} async-done(((f32[3,18432]{1,0:T(4,128)}), f32[3,18432]{1,0:T(4,128)}) %all-reduce.6.cloned.1.call-update) | async-done | bytes 221200 | tf_op jit(solution)/shard_map/psum | solution.py:123
  188.6 62.5 %all_gather.6 = f32[3,49152]{1,0:T(4,128)} all-gather(f32[3,384]{1,0:T(4,128)S(1)} %reshape.757), channel_id=1, replica_groups=mesh['gx'=32,'gy'=4] {'gx','gy'}, dimensions={1}, use_global_device_ids=true | all-gather | bytes 594432 | tf_op jit(solution)/shard_map/all_gather | solution.py:117
  253.6 2.6 copy.42
  263.1 4.9 collective-permute-start.3
  268.0 4.9 fusion.3
  275.2 6.7 %scatter_fusion = f32[3,2048,128]{2,0,1:T(4,128)} fusion(f32[3,2048,128]{2,0,1:T(4,128)} %broadcast.918.clone, s32[64]{0:T(128)S(1)} %copy-done.29, f32[64,3,128]{2,1,0:T(4,128)S(1)} %bitcast.124), kind=kCustom, calls=%fused_computation.8 | custom fusion | flops 24576 | bytes 295168 | tf_op jit(solution)/shard_map/scatter-add | solution.py:131
  281.9 4.1 copy.43
  286.0 4.8 reshape.760
  290.9 4.4 select_maximum_fusion.4
  295.3 5.1 fusion.18
  303.5 6.5 %copy.44 = f32[3,2048,128]{2,0,1:T(4,128)} copy(f32[3,2048,128]{2,1,0:T(8,128)} %reshape.761) | data formatting | bytes 6291456 | tf_op jit(solution)/shard_map/reshape | solution.py:103
  310.0 2.8 gather_fusion.5
  312.9 6.0 %fusion.43 = f32[3,4,192]{2,0,1:T(4,128)S(1)} fusion(f32[3,4,16,128]{3,0,2,1:T(4,128)S(1)} %bitcast.121, f32[4]{0:T(128)S(1)} %copy-done.33, f32[4,192]{1,0:T(4,128)S(1)} %bitcast.132, f32[4,16,128]{2,1,0:T(8,128)S(1)} %copy-done.16, f32[4,16,192]{2,1,0:T(8,128)S(1)} %copy-done.13), kind=kOutput, calls=%fused_computation.81 | convolution fusion | flops 64487424 | bytes 192528 | tf_op jit(solution)/shard_map/htcp,khtc->khp/dot_general | solution.py:104
  318.9 3.2 collective-permute-start.4
  332.1 4.7 collective-permute-start.7
  336.8 138.6 %all-reduce.8.cloned.1.call-done = (f32[3,18432]{1,0:T(4,128)}, f32[3,18432]{1,0:T(4,128)}) async-done(((f32[3,18432]{1,0:T(4,128)}, f32[3,18432]{1,0:T(4,128)}), (f32[3,18432]{1,0:T(4,128)}, f32[3,18432]{1,0:T(4,128)})) %all-reduce.8.cloned.1.call-update) | async-done | bytes 442384 | tf_op jit(solution)/shard_map/psum | solution.py:123
  482.4 62.0 %all_gather.7 = f32[3,49152]{1,0:T(4,128)} all-gather(f32[3,384]{1,0:T(4,128)S(1)} %reshape.763), channel_id=1, replica_groups=mesh['gx'=32,'gy'=4] {'gx','gy'}, dimensions={1}, use_global_device_ids=true | all-gather | bytes 594432 | tf_op jit(solution)/shard_map/all_gather | solution.py:117
  552.1 6.0 fusion.1
  560.3 7.1 %scatter_fusion.1 = f32[3,2048,128]{2,0,1:T(4,128)} fusion(f32[3,2048,128]{2,0,1:T(4,128)} %broadcast.918, s32[64]{0:T(128)S(1)} %copy-done.30, f32[64,3,128]{2,1,0:T(4,128)} %bitcast.123), kind=kCustom, calls=%fused_computation.9 | custom fusion | flops 24576 | bytes 295168 | tf_op jit(solution)/shard_map/scatter-add | solution.py:131
  567.3 4.1 copy.48
  571.4 4.5 reshape.766
  578.1 5.4 select_maximum_fusion
  583.6 5.5 fusion.10
  (158 shorter events, 68.9 us)
Async XLA Ops:
  7.2 175.8 %all-reduce.6.cloned.1.call-start = ((), (), s32[]{:S(2)}) async-start(), calls=%async_computation | async-start | bytes 589824 | tf_op jit(solution)/shard_map/psum | solution.py:123
  9.8 60.4 %copy-start.21 = (pred[4,96]{1,0:T(4,128)(4,1)}, pred[4,96]{1,0:T(4,128)(4,1)S(1)}, u32[]{:S(2)}) copy-start(pred[4,96]{1,0:T(4,128)(4,1)S(1)} %get-tuple-element.9) | copy-start | bytes 1156
  10.6 17.9 %copy-start.31 = (f32[4]{0:T(128)}, f32[4]{0:T(128)S(1)}, u32[]{:S(2)}) copy-start(f32[4]{0:T(128)S(1)} %broadcast_select_fusion) | copy-start | bytes 52
  12.5 16.0 %copy-start.26 = (f32[1,4,192]{2,1,0:T(4,128)}, f32[1,4,192]{2,1,0:T(4,128)S(1)}, u32[]{:S(2)}) copy-start(f32[1,4,192]{2,1,0:T(4,128)S(1)} %copy.69) | copy-start | bytes 9220
  12.6 51.6 %copy-start.14 = (f32[4,16,128]{2,1,0:T(8,128)}, f32[4,16,128]{2,1,0:T(8,128)S(1)}, u32[]{:S(2)}) copy-start(f32[4,16,128]{2,1,0:T(8,128)S(1)} %add_convert_fusion) | copy-start | bytes 98308
  28.5 35.7 %copy-start.11 = (f32[4,16,192]{2,1,0:T(8,128)}, f32[4,16,192]{2,1,0:T(8,128)S(1)}, u32[]{:S(2)}) copy-start(f32[4,16,192]{2,1,0:T(8,128)S(1)} %multiply_add_fusion) | copy-start | bytes 147460
  37.8 437.6 %all-reduce.8.cloned.1.call-start = ((), (), s32[]{:S(2)}) async-start(), calls=%async_computation.1 | async-start | bytes 1179648 | tf_op jit(solution)/shard_map/psum | solution.py:123
  38.7 219.5 %collective-permute-start.1 = (f32[3,1,16,1024]{3,2,1,0:T(8,128)}, f32[3,1,16,1024]{3,2,1,0:T(8,128)}, u32[]{:S(2)}, u32[]{:S(2)}) collective-permute-start(f32[3,1,16,1024]{3,2,1,0:T(8,128)} %get-tuple-element.17), channel_id=1, source_target_pairs={{0,4},{4,8},{8,12},{12,16},{16,20},{20,24},{24,28},{28,32},{32,36}... | collective-permute-start | bytes 589832 | tf_op jit(solution)/shard_map/ppermute | solution.py:24
  43.6 215.7 %collective-permute-start = (f32[3,1,16,1024]{3,2,1,0:T(8,128)}, f32[3,1,16,1024]{3,2,1,0:T(8,128)}, u32[]{:S(2)}, u32[]{:S(2)}) collective-permute-start(f32[3,1,16,1024]{3,2,1,0:T(8,128)} %get-tuple-element.16), channel_id=1, source_target_pairs={{4,0},{8,4},{12,8},{16,12},{20,16},{24,20},{28,24},{32,28},{36,32}... | collective-permute-start | bytes 589832 | tf_op jit(solution)/shard_map/ppermute | solution.py:26
  47.0 14.3 %copy-start.24 = (s32[96]{0:T(128)}, s32[96]{0:T(128)S(1)}, u32[]{:S(2)}) copy-start(s32[96]{0:T(128)S(1)} %convert_reduce_fusion) | copy-start | bytes 1156
  54.8 9.4 %copy-start.27 = (f32[1,4,192]{2,1,0:T(4,128)S(1)}, f32[1,4,192]{2,1,0:T(4,128)}, u32[]{:S(2)}) copy-start(f32[1,4,192]{2,1,0:T(4,128)} %copy-done.26) | copy-start | bytes 9220
  54.8 9.4 %copy-start.32 = (f32[4]{0:T(128)S(1)}, f32[4]{0:T(128)}, u32[]{:S(2)}) copy-start(f32[4]{0:T(128)} %copy-done.31) | copy-start | bytes 52
  73.5 185.8 %copy-start.23 = (s32[1024]{0:T(1024)}, s32[1024]{0:T(1024)S(1)}, u32[]{:S(2)}) copy-start(s32[1024]{0:T(1024)S(1)} %pad_clamp_fusion) | copy-start | bytes 12292
  256.3 11.7 %copy-start.12 = (f32[4,16,192]{2,1,0:T(8,128)S(1)}, f32[4,16,192]{2,1,0:T(8,128)}, u32[]{:S(2)}) copy-start(f32[4,16,192]{2,1,0:T(8,128)} %copy-done.11) | copy-start | bytes 147460
  256.3 11.7 %copy-start.15 = (f32[4,16,128]{2,1,0:T(8,128)S(1)}, f32[4,16,128]{2,1,0:T(8,128)}, u32[]{:S(2)}) copy-start(f32[4,16,128]{2,1,0:T(8,128)} %copy-done.14) | copy-start | bytes 98308
  256.3 11.7 %copy-start.28 = (f32[1,4,192]{2,1,0:T(4,128)S(1)}, f32[1,4,192]{2,1,0:T(4,128)}, u32[]{:S(2)}) copy-start(f32[1,4,192]{2,1,0:T(4,128)} %copy-done.26) | copy-start | bytes 9220
  256.3 11.7 %copy-start.33 = (f32[4]{0:T(128)S(1)}, f32[4]{0:T(128)}, u32[]{:S(2)}) copy-start(f32[4]{0:T(128)} %copy-done.31) | copy-start | bytes 52
  260.3 12.7 %copy-start.2 = (f32[3,18,16,1024]{3,2,1,0:T(8,128)}, f32[3,18,16,1024]{3,2,1,0:T(8,128)S(1)}, u32[]{:S(2)}) copy-start(f32[3,18,16,1024]{3,2,1,0:T(8,128)S(1)} %constant_dynamic-update-slice_fusion) | copy-start | bytes 10616836
  261.8 29.0 %collective-permute-start.2 = (f32[3,18,1,1024]{3,2,1,0:T(1,128)}, f32[3,18,1,1024]{3,2,1,0:T(1,128)}, u32[]{:S(2)}, u32[]{:S(2)}) collective-permute-start(f32[3,18,1,1024]{3,2,1,0:T(1,128)} %get-tuple-element.13), channel_id=1, source_target_pairs={{1,0},{2,1},{3,2},{5,4},{6,5},{7,6},{9,8},{10,9},{11,10},{13,12},{... | collective-permute-start | bytes 663560 | tf_op jit(solution)/shard_map/ppermute | solution.py:26
  263.1 27.7 %collective-permute-start.3 = (f32[3,18,1,1024]{3,2,1,0:T(1,128)}, f32[3,18,1,1024]{3,2,1,0:T(1,128)}, u32[]{:S(2)}, u32[]{:S(2)}) collective-permute-start(f32[3,18,1,1024]{3,2,1,0:T(1,128)} %get-tuple-element.12), channel_id=1, source_target_pairs={{0,1},{1,2},{2,3},{4,5},{5,6},{6,7},{8,9},{9,10},{10,11},{12,13},{... | collective-permute-start | bytes 663560 | tf_op jit(solution)/shard_map/ppermute | solution.py:24
  302.7 10.2 %copy-start.13 = (f32[4,16,192]{2,1,0:T(8,128)S(1)}, f32[4,16,192]{2,1,0:T(8,128)}, u32[]{:S(2)}) copy-start(f32[4,16,192]{2,1,0:T(8,128)} %copy-done.11) | copy-start | bytes 147460
  302.7 10.2 %copy-start.16 = (f32[4,16,128]{2,1,0:T(8,128)S(1)}, f32[4,16,128]{2,1,0:T(8,128)}, u32[]{:S(2)}) copy-start(f32[4,16,128]{2,1,0:T(8,128)} %copy-done.14) | copy-start | bytes 98308
  312.9 11.7 %copy-start.22 = (pred[4,96]{1,0:T(4,128)(4,1)S(1)}, pred[4,96]{1,0:T(4,128)(4,1)}, u32[]{:S(2)}) copy-start(pred[4,96]{1,0:T(4,128)(4,1)} %copy-done.21) | copy-start | bytes 1156
  318.9 160.9 %copy-start.18 = (f32[2,192]{1,0:T(2,128)S(1)}, f32[2,192]{1,0:T(2,128)}, u32[]{:S(2)}) copy-start(f32[2,192]{1,0:T(2,128)} %mul.189) | copy-start | bytes 4612
  318.9 160.9 %copy-start.19 = (pred[96]{0:T(512)(128)(4,1)S(1)}, pred[96]{0:T(512)(128)(4,1)}, u32[]{:S(2)}) copy-start(pred[96]{0:T(512)(128)(4,1)} %get-tuple-element.25) | copy-start | bytes 292
  318.9 10.6 %collective-permute-start.4 = (f32[3,1,16,1024]{3,2,1,0:T(8,128)}, f32[3,1,16,1024]{3,2,1,0:T(8,128)S(1)}, u32[]{:S(2)}, u32[]{:S(2)}) collective-permute-start(f32[3,1,16,1024]{3,2,1,0:T(8,128)} %get-tuple-element.15), channel_id=1, source_target_pairs={{4,0},{8,4},{12,8},{16,12},{20,16},{24,20},{28,24},{32,28},{36,32}... | collective-permute-start | bytes 589832 | tf_op jit(solution)/shard_map/ppermute | solution.py:26
  322.1 7.4 %collective-permute-start.5 = (f32[3,1,16,1024]{3,2,1,0:T(8,128)}, f32[3,1,16,1024]{3,2,1,0:T(8,128)S(1)}, u32[]{:S(2)}, u32[]{:S(2)}) collective-permute-start(f32[3,1,16,1024]{3,2,1,0:T(8,128)} %get-tuple-element.14), channel_id=1, source_target_pairs={{0,4},{4,8},{8,12},{12,16},{16,20},{20,24},{24,28},{28,32},{32,36}... | collective-permute-start | bytes 589832 | tf_op jit(solution)/shard_map/ppermute | solution.py:24
  329.5 145.8 %copy-start.7 = (f32[3,1,16,1024]{3,2,1,0:T(8,128)}, f32[3,1,16,1024]{3,2,1,0:T(8,128)S(1)}, u32[]{:S(2)}) copy-start(f32[3,1,16,1024]{3,2,1,0:T(8,128)S(1)} %collective-permute-done.4) | copy-start | bytes 589828
  329.6 145.8 %copy-start.9 = (f32[3,1,16,1024]{3,2,1,0:T(8,128)}, f32[3,1,16,1024]{3,2,1,0:T(8,128)S(1)}, u32[]{:S(2)}) copy-start(f32[3,1,16,1024]{3,2,1,0:T(8,128)S(1)} %collective-permute-done.5) | copy-start | bytes 589828
  330.8 247.3 %collective-permute-start.6 = (f32[3,18,1,1024]{3,2,1,0:T(1,128)}, f32[3,18,1,1024]{3,2,1,0:T(1,128)}, u32[]{:S(2)}, u32[]{:S(2)}) collective-permute-start(f32[3,18,1,1024]{3,2,1,0:T(1,128)} %get-tuple-element.11), channel_id=1, source_target_pairs={{1,0},{2,1},{3,2},{5,4},{6,5},{7,6},{9,8},{10,9},{11,10},{13,12},{... | collective-permute-start | bytes 663560 | tf_op jit(solution)/shard_map/ppermute | solution.py:26
  332.1 246.0 %collective-permute-start.7 = (f32[3,18,1,1024]{3,2,1,0:T(1,128)}, f32[3,18,1,1024]{3,2,1,0:T(1,128)}, u32[]{:S(2)}, u32[]{:S(2)}) collective-permute-start(f32[3,18,1,1024]{3,2,1,0:T(1,128)} %get-tuple-element.10), channel_id=1, source_target_pairs={{0,1},{1,2},{2,3},{4,5},{5,6},{6,7},{8,9},{9,10},{10,11},{12,13},{... | collective-permute-start | bytes 663560 | tf_op jit(solution)/shard_map/ppermute | solution.py:24
  475.3 76.7 %copy-start.17 = (f32[4,16,128]{2,1,0:T(8,128)S(1)}, f32[4,16,128]{2,1,0:T(8,128)}, u32[]{:S(2)}) copy-start(f32[4,16,128]{2,1,0:T(8,128)} %copy-done.14) | copy-start | bytes 98308
  (12 other events, 60.2 us)
Sparse Core Ops, SparseCore 0:
  37.9 144.9 all-reduce.5
  329.6 145.6 all-reduce.7
where the time goes:
time: 604 us; the launch traced here: 596 us
  waiting for transfers between devices  248 us (41%)
  blocking collectives  124 us (21%)
  local copies, waits for them, and re-layouts  105 us (17%)
  other arithmetic  44.8 us (7%)
  matrix products  33.8 us (6%)
  starting transfers between devices  25.2 us (4%)
  between operations  14.9 us (2%)
    psum x2, waiting for transfers between devices, substep(): lax.psum(sample(velocity_now), ('gx', 'gy')).reshape(3, rotors, points_n)  248 us
    all_gather x2, blocking collectives, hosted_force(): lax.all_gather(owned_force.reshape(3, own_max * points_n), ('gx', 'gy'),...  124 us
    reshape x6, local copies, waits for them, and re-layouts, local_sample(): gathered = field_in.reshape(3, cx_n * cy_n * tiles_z, 128)[:, local_tiles]  32.6 us
    dot_general x3, matrix products, local_sample(): jnp.einsum('htcp,khtc->khp', kernel, gathered, precision=lax.Precision.HI...  18 us
    ppermute x4, starting transfers between devices, extended(): lax.ppermute(tail, axis, [(i, (i + 1) % count) for i in range(ends)])  16.9 us
    scatter-add x2, other arithmetic, substep(): forcing.at[:, flat_local].add(contrib.reshape(3, -1, 128))  13.8 us
  transfers between devices with their start and end apart: 10, of which 2 were waited for; matrix products, arithmetic and copies ran while one was open for 19% of the time, Pallas kernels for 0%

commit v1 on v0

v1 whole, which is shorter than its diff:
```python
import functools
import math

import jax
import jax.numpy as jnp
from jax import lax
from jax.experimental import pallas as pl
from jax.experimental.pallas import tpu as pltpu
from jax.sharding import PartitionSpec as P

AXES = ("gx", "gy")
HOST_MAX = 4
BOX = 4
LANES = 256
FIELDS = 8

gauss_norm = math.pi ** (-1.5)
time_step = 0.5
viscosity = 0.15
HIGH = lax.Precision.HIGHEST

VMEM = pl.BlockSpec(memory_space=pltpu.VMEM)
SMEM = pl.BlockSpec(memory_space=pltpu.SMEM)
HBM = pl.BlockSpec(memory_space=pl.ANY)
PARAMS = pltpu.CompilerParams(vmem_limit_bytes=48 * 2**20)


def log2(value):
    bits = value.bit_length() - 1
    assert 1 << bits == value
    return bits


def gaussians(points, first_i, first_j, first_z, valid):
    cell_z = lax.broadcasted_iota(jnp.int32, (128, LANES), 0) + first_z
    delta_z = cell_z.astype(jnp.float32) - points[2:3]
    along_z = jnp.where(valid, gauss_norm * jnp.exp(-(delta_z * delta_z)), 0.0)
    tile = lax.broadcasted_iota(jnp.int32, (BOX * BOX, LANES), 0)
    delta_x = (lax.shift_right_logical(tile, 2) + first_i).astype(jnp.float32) - points[0:1]
    delta_y = ((tile & 3) + first_j).astype(jnp.float32) - points[1:2]
    across = jnp.exp(-(delta_x * delta_x + delta_y * delta_y))
    return along_z, across


def valid_lanes(odd, points_n):
    lane = lax.broadcasted_iota(jnp.int32, (1, LANES), 1)
    first = odd * (LANES - points_n)
    return (lane >= first) & (lane < first + points_n)


def rotor_at(info_ref, h):
    return [info_ref[h * FIELDS + f] for f in range(FIELDS)]


def reduce_tiles(product, across, k):
    rows = product[k * BOX * BOX : (k + 1) * BOX * BOX]
    return jnp.sum(rows * across, axis=0, keepdims=True)


def sample_kernel(
    rotors, cx_n, cy_n, tiles_z, full_y, points_n, n_gy,
    meta_ref, points_ref, motion_ref, velocity_ref, cotangent_ref,
    info_ref, terms_ref,
    seen_ref, point_ref, move_ref, block_ref, cell_ref, sems,
):
    log_t, log_y = log2(tiles_z), log2(full_y)
    log_cx, log_cy = log2(cx_n), log2(cy_n)
    gx, gy = meta_ref[2 * rotors], meta_ref[2 * rotors + 1]

    def clear(d, carry):
        seen_ref[d] = 0
        return carry

    lax.fori_loop(0, seen_ref.shape[0], clear, 0, unroll=16)

    def visit(r, count):
        tile = meta_ref[r]
        i = lax.shift_right_logical(tile, log_t + log_y)
        j = lax.shift_right_logical(tile, log_t) & (full_y - 1)
        mine = (lax.shift_right_logical(i, log_cx) == gx) & (lax.shift_right_logical(j, log_cy) == gy)
        own = meta_ref[rotors + r]
        earlier = seen_ref[own]
        seen_ref[own] = earlier + 1

        @pl.when(mine)
        def _():
            base = count * FIELDS
            info_ref[base] = r
            info_ref[base + 1] = i
            info_ref[base + 2] = j
            info_ref[base + 3] = tile & (tiles_z - 1)
            info_ref[base + 4] = own
            info_ref[base + 5] = earlier

        return count + mine.astype(jnp.int32)

    count = lax.fori_loop(0, rotors, visit, jnp.int32(0), unroll=8)
    info_ref[HOST_MAX * FIELDS] = count

    def copies(h):
        r, i, j, kz, _, _, _, _ = rotor_at(info_ref, h)
        start = lax.shift_right_logical(r, 1) * (2 * points_n) + (r & 1) * 128
        lanes = pl.ds(pl.multiple_of(start, 128), LANES)
        cells = pl.ds(pl.multiple_of(kz * 128, 128), 128)
        planes = pl.ds(i & (cx_n - 1), BOX)
        return [
            pltpu.make_async_copy(points_ref.at[:, lanes], point_ref.at[h], sems.at[h, 0]),
            pltpu.make_async_copy(motion_ref.at[:, lanes], move_ref.at[h], sems.at[h, 1]),
            pltpu.make_async_copy(velocity_ref.at[:, planes, :, cells], block_ref.at[h, 0], sems.at[h, 2]),
            pltpu.make_async_copy(cotangent_ref.at[:, planes, :, cells], block_ref.at[h, 1], sems.at[h, 3]),
        ]

    for h in range(HOST_MAX):

        @pl.when(h < count)
        def _(h=h):
            for copy in copies(h):
                copy.start()

    for h in range(HOST_MAX):

        @pl.when(h < count)
        def _(h=h):
            for copy in copies(h):
                copy.wait()
            r, i, j, kz, _, _, _, _ = rotor_at(info_ref, h)
            points = point_ref[h]
            along_z, across = gaussians(points, i, j, kz * 128, valid_lanes(r & 1, points_n))
            rows = pl.ds(j & (cy_n - 1), BOX)
            for field in range(2):
                for k in range(3):
                    for a in range(BOX):
                        at = ((field * 3 + k) * BOX + a) * BOX
                        cell_ref[at : at + BOX, :] = block_ref[h, field, k, a, rows, :]
            product = jnp.dot(cell_ref[...], along_z, precision=HIGH, preferred_element_type=jnp.float32)
            move = move_ref[h]
            relative = [reduce_tiles(product, across, k) - move[k : k + 1] for k in range(3)]
            speed = jnp.sqrt(sum(v * v for v in relative))
            for k in range(3):
                terms_ref[h, k : k + 1, :] = speed * relative[k]
                terms_ref[h, 3 + k : 4 + k, :] = reduce_tiles(product, across, 3 + k)
                terms_ref[h, 6 + k : 7 + k, :] = points[k : k + 1]
                terms_ref[h, 9 + k : 10 + k, :] = move[k : k + 1]


def spread(along_z, across, force, cells_ref, block_ref, i, j, kz):
    weighted = jnp.concatenate([across * force[k] for k in range(3)], axis=0)
    contrib = lax.dot_general(
        weighted, along_z, (((1,), (1,)), ((), ())), precision=HIGH, preferred_element_type=jnp.float32
    )
    where = (slice(None), pl.ds(i, BOX), slice(None), pl.ds(pl.multiple_of(kz * 128, 128), 128))
    block_ref[...] = cells_ref[where]
    for k in range(3):
        for a in range(BOX):
            at = (k * BOX + a) * BOX
            rows = (k, a, pl.ds(j, BOX))
            block_ref[rows] = block_ref[rows] + time_step * contrib[at : at + BOX]
    cells_ref[where] = block_ref[...]


def force_kernel(
    cx_n, cy_n, points_n,
    info_ref, terms_ref, table_ref, start_ref,
    mid_ref, x_low_ref, x_high_ref, y_low_ref, y_high_ref, send_ref, force_ref,
    cell_ref, block_ref,
):
    count = info_ref[HOST_MAX * FIELDS]
    mid_ref[...] = start_ref[...]
    send_ref[...] = jnp.zeros_like(send_ref)

    def setup(h):
        r, i, j, kz, own, rank, _, _ = rotor_at(info_ref, h)
        points = terms_ref[h, 6:9, :]
        along_z, across = gaussians(points, i, j, kz * 128, valid_lanes(r & 1, points_n))
        here = (i & (cx_n - 1), j & (cy_n - 1), kz)
        row = table_ref[pl.ds(own, 1), :]
        coef = jnp.where(rank > 0, row[:, 128:], row[:, :LANES])
        shifted_up = pltpu.roll(coef, LANES - points_n, 1)
        shifted_down = pltpu.roll(coef, points_n, 1)
        odd = r & 1
        coef = jnp.where(rank == odd, coef, jnp.where(rank < odd, shifted_up, shifted_down))
        return along_z, across, here, coef, odd, own, rank

    for h in range(HOST_MAX):

        @pl.when(h < count)
        def _(h=h):
            along_z, across, here, coef, _, _, _ = setup(h)
            force = [coef * terms_ref[h, k : k + 1, :] for k in range(3)]
            spread(along_z, across, force, mid_ref, block_ref, *here)

    for h in range(HOST_MAX):

        @pl.when(h < count)
        def _(h=h):
            along_z, across, (i, j, kz), coef, odd, own, rank = setup(h)
            cells = pl.ds(pl.multiple_of(kz * 128, 128), 128)
            block_ref[...] = mid_ref[:, pl.ds(i, BOX), :, cells]
            for k in range(3):
                for a in range(BOX):
                    at = (k * BOX + a) * BOX
                    cell_ref[at : at + BOX, :] = block_ref[k, a, pl.ds(j, BOX)]
            product = jnp.dot(cell_ref[...], along_z, precision=HIGH, preferred_element_type=jnp.float32)
            relative = [reduce_tiles(product, across, k) - terms_ref[h, 9 + k : 10 + k, :] for k in range(3)]
            speed = jnp.sqrt(sum(v * v for v in relative))
            grad = jnp.zeros((1, LANES), jnp.float32)
            for k in range(3):
                shape_term = speed * relative[k]
                grad = grad + terms_ref[h, 3 + k : 4 + k, :] * shape_term
                force_ref[h, k : k + 1, :] = coef * shape_term
            for k in range(3):
                force_ref[h, 3 + k : 4 + k, :] = terms_ref[h, 6 + k : 7 + k, :]
            grad = time_step * grad
            shifted_up = pltpu.roll(grad, LANES - points_n, 1)
            shifted_down = pltpu.roll(grad, points_n, 1)
            grad = jnp.where(rank == odd, grad, jnp.where(odd < rank, shifted_up, shifted_down))
            blank = jnp.zeros((1, 128), jnp.float32)
            wide = jnp.where(
                rank > 0, jnp.concatenate([blank, grad], axis=1), jnp.concatenate([grad, blank], axis=1)
            )
            send_ref[pl.ds(own, 1), :] = send_ref[pl.ds(own, 1), :] + wide

    x_low_ref[...] = mid_ref[:, 0]
    x_high_ref[...] = mid_ref[:, cx_n - 1]
    for x in range(cx_n):
        y_low_ref[:, x : x + 1] = mid_ref[:, x, 0:1]
        y_high_ref[:, x : x + 1] = mid_ref[:, x, cy_n - 1 : cy_n]


def substep_kernel(
    cx_n, cy_n, cz_n, points_n, n_gx, n_gy, gx_at, forced,
    *refs,
):
    if forced:
        meta_ref, info_ref, force_ref, now_ref, x_low_ref, x_high_ref, y_low_ref, y_high_ref, next_ref, block_ref = refs
    else:
        meta_ref, now_ref, x_low_ref, x_high_ref, y_low_ref, y_high_ref, next_ref = refs
    gx, gy = meta_ref[gx_at], meta_ref[gx_at + 1]
    row = lax.broadcasted_iota(jnp.int32, (cy_n, cz_n), 0)
    lane = lax.broadcasted_iota(jnp.int32, (cy_n, cz_n), 1)
    rate = time_step * viscosity
    has_x_low = (gx > 0).astype(jnp.float32)
    has_x_high = (gx < n_gx - 1).astype(jnp.float32)
    has_y_low = (gy > 0).astype(jnp.float32)
    has_y_high = (gy < n_gy - 1).astype(jnp.float32)

    def plane(x, below, above, k):
        now = now_ref[k, x]
        y_below = jnp.where(row == 0, y_low_ref[k, pl.ds(x, 1)] * has_y_low, pltpu.roll(now, 1, 0))
        y_above = jnp.where(
            row == cy_n - 1, y_high_ref[k, pl.ds(x, 1)] * has_y_high, pltpu.roll(now, cy_n - 1, 0)
        )
        z_below = jnp.where(lane == 0, 0.0, pltpu.roll(now, 1, 1))
        z_above = jnp.where(lane == cz_n - 1, 0.0, pltpu.roll(now, cz_n - 1, 1))
        total = (below + above) + (y_below + y_above) + (z_below + z_above)
        next_ref[k, x] = now + rate * (total - 6.0 * now)

    for k in range(3):
        plane(0, x_low_ref[k] * has_x_low, now_ref[k, 1], k)
        plane(cx_n - 1, now_ref[k, cx_n - 2], x_high_ref[k] * has_x_high, k)

        def inner(x, carry, k=k):
            plane(x, now_ref[k, x - 1], now_ref[k, x + 1], k)
            return carry

        lax.fori_loop(1, cx_n - 1, inner, 0)

    if forced:
        count = info_ref[HOST_MAX * FIELDS]
        for h in range(HOST_MAX):

            @pl.when(h < count)
            def _(h=h):
                r, i, j, kz, _, _, _, _ = rotor_at(info_ref, h)
                along_z, across = gaussians(
                    force_ref[h, 3:6, :], i, j, kz * 128, valid_lanes(r & 1, points_n)
                )
                force = [force_ref[h, k : k + 1, :] for k in range(3)]
                spread(along_z, across, force, next_ref, block_ref, i & (cx_n - 1), j & (cy_n - 1), kz)


def ring(count, step):
    return [(i, (i + step) % count) for i in range(count)]


def exchange(faces, n_gx, n_gy):
    x_low, x_high, y_low, y_high = faces
    return (
        lax.ppermute(x_high, "gx", ring(n_gx, 1)),
        lax.ppermute(x_low, "gx", ring(n_gx, -1)),
        lax.ppermute(y_high, "gy", ring(n_gy, 1)),
        lax.ppermute(y_low, "gy", ring(n_gy, -1)),
    )


def per_device(velocity, cotangent, points, motion, coef, readers, owner):
    _, cx_n, cy_n, cz_n = velocity.shape
    tiles_z = cz_n // 128
    n_gx, n_gy = lax.axis_size("gx"), lax.axis_size("gy")
    devices = n_gx * n_gy
    full_y = cy_n * n_gy
    rotors = readers.shape[0]
    points_n = points.shape[1] // rotors
    own_n = coef.shape[0]
    f32 = jnp.float32

    meta = jnp.concatenate(
        [readers[:, 0], owner, lax.axis_index("gx")[None], lax.axis_index("gy")[None]]
    ).astype(jnp.int32)
    table = lax.all_to_all(jnp.broadcast_to(coef[None], (devices, own_n)), AXES, 0, 0, tiled=True)
    faces = (velocity[:, 0], velocity[:, cx_n - 1], velocity[:, :, 0], velocity[:, :, cy_n - 1])
    halos = exchange(faces, n_gx, n_gy)

    info, terms = pl.pallas_call(
        functools.partial(sample_kernel, rotors, cx_n, cy_n, tiles_z, full_y, points_n, n_gy),
        out_shape=(
            jax.ShapeDtypeStruct((64,), jnp.int32),
            jax.ShapeDtypeStruct((HOST_MAX, 16, LANES), f32),
        ),
        in_specs=[SMEM, HBM, HBM, HBM, HBM],
        out_specs=(SMEM, VMEM),
        scratch_shapes=[
            pltpu.SMEM((devices,), jnp.int32),
            pltpu.VMEM((HOST_MAX, 3, LANES), f32),
            pltpu.VMEM((HOST_MAX, 3, LANES), f32),
            pltpu.VMEM((HOST_MAX, 2, 3, BOX, cy_n, 128), f32),
            pltpu.VMEM((6 * BOX * BOX, 128), f32),
            pltpu.SemaphoreType.DMA((HOST_MAX, 4)),
        ],
        compiler_params=PARAMS,
        name="sample",
    )(meta, points, motion, velocity, cotangent)

    def substep(now, halos, extra):
        return pl.pallas_call(
            functools.partial(
                substep_kernel, cx_n, cy_n, cz_n, points_n, n_gx, n_gy, 2 * rotors, bool(extra)
            ),
            out_shape=jax.ShapeDtypeStruct(velocity.shape, f32),
            in_specs=[SMEM] + ([SMEM, VMEM] if extra else []) + [VMEM] * 5,
            out_specs=VMEM,
            scratch_shapes=[pltpu.VMEM((3, BOX, cy_n, 128), f32)] if extra else [],
            compiler_params=PARAMS,
            name="substep",
        )(meta, *extra, now, *halos)

    start = substep(velocity, halos, ())
    face_x = jax.ShapeDtypeStruct((3, cy_n, cz_n), f32)
    face_y = jax.ShapeDtypeStruct((3, cx_n, cz_n), f32)
    mid, x_low, x_high, y_low, y_high, send, force = pl.pallas_call(
        functools.partial(force_kernel, cx_n, cy_n, points_n),
        out_shape=(
            jax.ShapeDtypeStruct(velocity.shape, f32), face_x, face_x, face_y, face_y,
            jax.ShapeDtypeStruct((devices, own_n), f32),
            jax.ShapeDtypeStruct((HOST_MAX, 8, LANES), f32),
        ),
        in_specs=[SMEM, VMEM, VMEM, VMEM],
        out_specs=(VMEM,) * 7,
        scratch_shapes=[
            pltpu.VMEM((3 * BOX * BOX, 128), f32),
            pltpu.VMEM((3, BOX, cy_n, 128), f32),
        ],
        compiler_params=PARAMS,
        name="force",
    )(info, terms, table, start)
    received = lax.all_to_all(send, AXES, 0, 0, tiled=True)
    halos = exchange((x_low, x_high, y_low, y_high), n_gx, n_gy)
    velocity_out = substep(mid, halos, (info, force))
    return velocity_out, jnp.sum(received, axis=0)


def solution(mesh):
    cells = P(None, "gx", "gy", None)
    return jax.shard_map(
        per_device,
        mesh=mesh,
        in_specs=(cells, cells, P(), P(), P(AXES), P(), P()),
        out_specs=(cells, P(AXES)),
        check_vma=False,
    )
```

time: 604 us -> 79.5 us (0.13); the launches traced: 596 us -> 78.1 us
  waiting for transfers between devices: 248 us -> 0.02 us
  blocking collectives: 124 us -> 19.8 us
  local copies, waits for them, and re-layouts: 105 us -> 10.1 us
  other arithmetic: 44.8 us -> 2.41 us
  matrix products: 33.8 us -> 0 us
  Pallas kernels: 0 us -> 20 us
  between operations: 14.9 us -> 0.8 us
    psum x2 -> x0, waiting for transfers between devices: 248 us -> none  [substep(): lax.psum(sample(velocity_now), ('gx', 'gy')).reshape(3, rotors, points_n)]
    all_gather x2 -> x0, blocking collectives: 124 us -> none  [hosted_force(): lax.all_gather(owned_force.reshape(3, own_max * points_n), ('gx', 'gy'),...]
    reshape x20 -> x0, local copies, waits for them, and re-layouts: 60.9 us -> none  [the longest x6 32.6 us: local_sample(): gathered = field_in.reshape(3, cx_n * cy_n * tiles_z, 128)[:, local_tiles]]
    dot_general x11 -> x0, matrix products: 33.8 us -> none  [the longest x3 18 us: local_sample(): jnp.einsum('htcp,khtc->khp', kernel, gathered, precision=lax.Precision.HI...]
    pallas_call x0 -> x4, Pallas kernels: none -> 20 us  [the longest x2 14.5 us: substep(): pl.pallas_call(functools.partial(substep_kernel, cx_n, cy_n, cz_n, points...]
    all_to_all x0 -> x1, blocking collectives: none -> 19.8 us  [per_device(): received = lax.all_to_all(send, AXES, 0, 0, tiled=True)]
    gather x9 -> x0, local copies, waits for them, and re-layouts: 14.7 us -> none  [the longest x3 8.54 us: local_sample(): gathered = field_in.reshape(3, cx_n * cy_n * tiles_z, 128)[:, local_tiles]]
    scatter-add x2 -> x0, other arithmetic: 13.8 us -> none  [substep(): forcing.at[:, flat_local].add(contrib.reshape(3, -1, 128))]
  transfers between devices with their start and end apart: 10 -> 9, of which waited for: 2 -> 0; matrix products, arithmetic and copies ran while one was open for 19% -> 9% of each run, Pallas kernels for 0% -> 3%
where the time goes in v1:
time: 79.5 us; the launch traced here: 78.1 us
  starting transfers between devices  25 us (31%)
  Pallas kernels  20 us (25%)
  blocking collectives  19.8 us (25%)
  local copies, waits for them, and re-layouts  10.1 us (13%)
  other arithmetic  2.41 us (3%)
  between operations  0.8 us (1%)
    all_to_all x1, blocking collectives, per_device(): received = lax.all_to_all(send, AXES, 0, 0, tiled=True)  19.8 us
    pallas_call x2, Pallas kernels, substep(): pl.pallas_call(functools.partial(substep_kernel, cx_n, cy_n, cz_n, points...  14.5 us
    all_to_all x1, starting transfers between devices, per_device(): lax.all_to_all(jnp.broadcast_to(coef[None], (devices, own_n)), AXES, 0, 0...  11.5 us
    ppermute x2, starting transfers between devices, exchange(): lax.ppermute(x_low, 'gx', ring(n_gx, -1))  4.77 us
    unnamed x15, local copies, waits for them, and re-layouts  4.4 us
    ppermute x2, starting transfers between devices, exchange(): lax.ppermute(y_high, 'gy', ring(n_gy, 1))  4.16 us
    pallas_call x1, Pallas kernels, per_device(): pl.pallas_call(functools.partial(force_kernel, cx_n, cy_n, points_n), out...  3.14 us
    ppermute x2, starting transfers between devices, exchange(): lax.ppermute(y_low, 'gy', ring(n_gy, -1))  2.69 us
  transfers between devices with their start and end apart: 9, of which 0 were waited for; matrix products, arithmetic and copies ran while one was open for 9% of the time, Pallas kernels for 3%

profile of v1, /device:TPU:1, one launch (start us, length us, event | category | flops | bytes accessed | tf_op | source)
XLA Modules:
  0.0 78.1 jit_solution(6148008750113836866)
XLA Ops:
  0.7 1.5 %broadcast_in_dim.14 = f32[128,1,384]{2,1,0:T(1,128)} broadcast(f32[384]{0:T(512)} %param.11), dimensions={2} | broadcast | bytes 198144 | tf_op jit(solution)/shard_map/broadcast_in_dim | solution.py:310
  2.2 11.5 %all-to-all-start = ((f32[128,1,384]{2,1,0:T(1,128)}), f32[128,1,384]{2,1,0:T(1,128)S(1)}, u32[]{:S(2)}, u32[]{:S(2)}) async-start(f32[128,1,384]{2,1,0:T(1,128)} %broadcast_in_dim.14), calls=%async_computation | async-start | bytes 393216 | tf_op jit(solution)/shard_map/all_to_all | solution.py:310
  13.7 1.1 %slice_bitcast_fusion = (f32[3,16,1024]{2,1,0:T(8,128)S(1)}, f32[3,16,1024]{2,1,0:T(8,128)S(1)}) fusion(f32[3,16,16,1024]{3,2,1,0:T(8,128)} %refs_1_.1), kind=kLoop, calls=%fused_computation.3 | loop fusion | bytes 786432 | tf_op jit(solution)/shard_map/squeeze | solution.py:311
  14.7 1.1 %collective-permute-start.1 = (f32[3,16,1024]{2,1,0:T(8,128)S(1)}, f32[3,16,1024]{2,1,0:T(8,128)S(1)}, u32[]{:S(2)}, u32[]{:S(2)}) collective-permute-start(f32[3,16,1024]{2,1,0:T(8,128)S(1)} %get-tuple-element.22), channel_id=1, source_target_pairs={{0,124},{4,0},{8,4},{12,8},{16,12},{20,16},{24,20},{28,24},{32,28}... | collective-permute-start | bytes 589832 | tf_op jit(solution)/shard_map/ppermute | solution.py:290
  15.9 0.8 collective-permute-start
  16.6 2.3 %fusion = (f32[3,16,1,1024]{3,2,1,0:T(1,128)S(1)}, f32[3,16,1,1024]{3,2,1,0:T(1,128)S(1)}) fusion(f32[3,16,16,1024]{3,2,1,0:T(8,128)} %refs_1_.1), kind=kLoop, calls=%fused_computation.7 | loop fusion | bytes 786432 | tf_op jit(solution)/shard_map/slice | solution.py:311
  18.9 1.4 %collective-permute-start.2 = (f32[3,16,1024]{2,1,0:T(8,128)S(1)}, f32[3,16,1024]{2,1,0:T(8,128)S(1)}, u32[]{:S(2)}, u32[]{:S(2)}) collective-permute-start(f32[3,16,1024]{2,1,0:T(8,128)S(1)} %bitcast.24), channel_id=1, source_target_pairs={{0,1},{1,2},{2,3},{3,0},{4,5},{5,6},{6,7},{7,4},{8,9},{9,10},{10,1... | collective-permute-start | bytes 589832 | tf_op jit(solution)/shard_map/ppermute | solution.py:291
  20.4 1.4 %collective-permute-start.3 = (f32[3,16,1024]{2,1,0:T(8,128)S(1)}, f32[3,16,1024]{2,1,0:T(8,128)S(1)}, u32[]{:S(2)}, u32[]{:S(2)}) collective-permute-start(f32[3,16,1024]{2,1,0:T(8,128)S(1)} %bitcast.25), channel_id=1, source_target_pairs={{0,3},{1,0},{2,1},{3,2},{4,7},{5,4},{6,5},{7,6},{8,11},{9,8},{10,9... | collective-permute-start | bytes 589832 | tf_op jit(solution)/shard_map/ppermute | solution.py:292
  21.8 0.7 slice_bitcast_fusion.2
  22.5 0.7 pad_add_fusion.meta_ref.refs_0_
  23.2 0.0 copy-start
  23.2 1.9 %copy-done = f32[3,16,16,1024]{3,2,1,0:T(8,128)S(1)} copy-done((f32[3,16,16,1024]{3,2,1,0:T(8,128)S(1)}, f32[3,16,16,1024]{3,2,1,0:T(8,128)}, u32[]{:S(2)}) %copy-start) | copy-done | bytes 3145752
  25.1 2.3 %sample.1 = (s32[64]{0:T(128)S(1)}, f32[4,16,256]{2,1,0:T(8,128)S(1)}) custom-call(s32[194]{0:T(256)S(1)} %pad_add_fusion.meta_ref.refs_0_, f32[3,18432]{1,0:T(4,128)S(1)} %copy-done.2, f32[3,18432]{1,0:T(4,128)S(1)} %copy-done.3, f32[3,16,16,1024]{3,2,1,0:T(8,128)S(1)} %copy-done, f32[3,16,16,1024]{3,2,1,0:T(8,128)} %cotangent_ref.1), custom_call_target="tpu_custom_call" | custom-call | tf_op jit(solution)/shard_map/sample/pallas_call | solution.py:314
  27.4 0.0 all-to-all-done
  27.5 0.0 collective-permute-done.1.refs_3_
  27.5 0.0 collective-permute-done.refs_2_
  27.5 0.0 collective-permute-done.3.refs_5_
  27.5 6.9 %substep.2.start_ref = f32[3,16,16,1024]{3,2,1,0:T(8,128)S(1)} custom-call(s32[194]{0:T(256)S(1)} %pad_add_fusion.meta_ref.refs_0_, f32[3,16,16,1024]{3,2,1,0:T(8,128)} %refs_1_.1, f32[3,16,1024]{2,1,0:T(8,128)S(1)} %collective-permute-done.refs_2_, f32[3,16,1024]{2,1,0:T(8,128)S(1)} %collective-permute-done.1.refs_3_, ...), custom_call_target="tpu_custom_call" | custom-call | tf_op jit(solution)/shard_map/substep/pallas_call | solution.py:335
  34.4 0.0 copy-start.1
  34.4 1.7 %copy-done.1 = f32[3,16,16,1024]{3,2,1,0:T(8,128)} copy-done((f32[3,16,16,1024]{3,2,1,0:T(8,128)}, f32[3,16,16,1024]{3,2,1,0:T(8,128)S(1)}, u32[]{:S(2)}) %copy-start.1) | copy-done | bytes 3145752
  36.1 3.1 %force.1 = (f32[3,16,16,1024]{3,2,1,0:T(8,128)S(1)}, f32[3,16,1024]{2,1,0:T(8,128)}, f32[3,16,1024]{2,1,0:T(8,128)}, f32[3,16,1024]{2,1,0:T(8,128)}, f32[3,16,10...) custom-call(s32[64]{0:T(128)S(1)} %get-tuple-element.11.info_ref.refs_1_, ...), custom_call_target="tpu_custom_call" | custom-call | tf_op jit(solution)/shard_map/force/pallas_call | solution.py:350
  39.2 1.1 %collective-permute-start.4 = (f32[3,16,1024]{2,1,0:T(8,128)}, f32[3,16,1024]{2,1,0:T(8,128)S(1)}, u32[]{:S(2)}, u32[]{:S(2)}) collective-permute-start(f32[3,16,1024]{2,1,0:T(8,128)} %get-tuple-element.15), channel_id=1, source_target_pairs={{0,4},{4,8},{8,12},{12,16},{16,20},{20,24},{24,28},{28,32},{32,36}... | collective-permute-start | bytes 589832 | tf_op jit(solution)/shard_map/ppermute | solution.py:289
  40.3 3.6 %collective-permute-start.5 = (f32[3,16,1024]{2,1,0:T(8,128)}, f32[3,16,1024]{2,1,0:T(8,128)S(1)}, u32[]{:S(2)}, u32[]{:S(2)}) collective-permute-start(f32[3,16,1024]{2,1,0:T(8,128)} %get-tuple-element.16), channel_id=1, source_target_pairs={{0,124},{4,0},{8,4},{12,8},{16,12},{20,16},{24,20},{28,24},{32,28}... | collective-permute-start | bytes 589832 | tf_op jit(solution)/shard_map/ppermute | solution.py:290
  43.9 2.8 %collective-permute-start.6 = (f32[3,16,1024]{2,1,0:T(8,128)}, f32[3,16,1024]{2,1,0:T(8,128)}, u32[]{:S(2)}, u32[]{:S(2)}) collective-permute-start(f32[3,16,1024]{2,1,0:T(8,128)} %get-tuple-element.17), channel_id=1, source_target_pairs={{0,1},{1,2},{2,3},{3,0},{4,5},{5,6},{6,7},{7,4},{8,9},{9,10},{10,1... | collective-permute-start | bytes 589832 | tf_op jit(solution)/shard_map/ppermute | solution.py:291
  46.7 1.2 %collective-permute-start.7 = (f32[3,16,1024]{2,1,0:T(8,128)}, f32[3,16,1024]{2,1,0:T(8,128)}, u32[]{:S(2)}, u32[]{:S(2)}) collective-permute-start(f32[3,16,1024]{2,1,0:T(8,128)} %get-tuple-element.18), channel_id=1, source_target_pairs={{0,3},{1,0},{2,1},{3,2},{4,7},{5,4},{6,5},{7,6},{8,11},{9,8},{10,9... | collective-permute-start | bytes 589832 | tf_op jit(solution)/shard_map/ppermute | solution.py:292
  48.0 0.2 copy.17
  48.2 19.8 %all_to_all.17 = f32[128,1,384]{2,1,0:T(1,128)} all-to-all(f32[128,1,384]{2,1,0:T(1,128)S(1)} %copy.17), channel_id=1, replica_groups=mesh['gx'=32,'gy'=4] {'gx','gy'}, dimensions={0} | all-to-all | bytes 393216 | tf_op jit(solution)/shard_map/all_to_all | solution.py:366
  68.0 1.7 %reduce_sum.9 = f32[384]{0:T(512)} reduce(f32[128,1,384]{2,1,0:T(1,128)} %all_to_all.17, f32[]{:T(128)} %constant.10.clone.1), dimensions={0,1}, to_apply=%region_0.0 | reduce | flops 48768 | bytes 198148 | tf_op jit(solution)/shard_map/reduce_sum | solution.py:369
  69.7 0.0 collective-permute-done.6.refs_6_
  69.7 0.0 copy-start.5
  69.7 0.7 copy-done.5
  70.4 7.7 %substep.3 = f32[3,16,16,1024]{3,2,1,0:T(8,128)} custom-call(s32[194]{0:T(256)S(1)} %pad_add_fusion.meta_ref.refs_0_, s32[64]{0:T(128)S(1)} %get-tuple-element.11.info_ref.refs_1_, f32[4,8,256]{2,1,0:T(8,128)S(1)} %copy-done.5, f32[3,16,16,1024]{3,2,1,0:T(8,128)S(1)} %get-tuple-element.14.refs_3_, f32[3,16,1024]{2,1,0:T(8,128)S(1)} %collective-permute-done.4.refs_4_, ...), custom_call_target="tpu_custom_call" | custom-call | tf_op jit(solution)/shard_map/substep/pallas_call | solution.py:335
  (13 shorter events, 0.1 us)
Async XLA Ops:
  0.6 22.6 %copy-start.3 = (f32[3,18432]{1,0:T(4,128)S(1)}, f32[3,18432]{1,0:T(4,128)}, u32[]{:S(2)}) copy-start(f32[3,18432]{1,0:T(4,128)} %motion_ref.1) | copy-start | bytes 663556
  0.6 22.6 %copy-start.2 = (f32[3,18432]{1,0:T(4,128)S(1)}, f32[3,18432]{1,0:T(4,128)}, u32[]{:S(2)}) copy-start(f32[3,18432]{1,0:T(4,128)} %points_ref.1) | copy-start | bytes 663556
  2.2 25.3 %all-to-all-start = ((f32[128,1,384]{2,1,0:T(1,128)}), f32[128,1,384]{2,1,0:T(1,128)S(1)}, u32[]{:S(2)}, u32[]{:S(2)}) async-start(f32[128,1,384]{2,1,0:T(1,128)} %broadcast_in_dim.14), calls=%async_computation | async-start | bytes 393216 | tf_op jit(solution)/shard_map/all_to_all | solution.py:310
  14.7 12.8 %collective-permute-start.1 = (f32[3,16,1024]{2,1,0:T(8,128)S(1)}, f32[3,16,1024]{2,1,0:T(8,128)S(1)}, u32[]{:S(2)}, u32[]{:S(2)}) collective-permute-start(f32[3,16,1024]{2,1,0:T(8,128)S(1)} %get-tuple-element.22), channel_id=1, source_target_pairs={{0,124},{4,0},{8,4},{12,8},{16,12},{20,16},{24,20},{28,24},{32,28}... | collective-permute-start | bytes 589832 | tf_op jit(solution)/shard_map/ppermute | solution.py:290
  15.9 11.6 %collective-permute-start = (f32[3,16,1024]{2,1,0:T(8,128)S(1)}, f32[3,16,1024]{2,1,0:T(8,128)S(1)}, u32[]{:S(2)}, u32[]{:S(2)}) collective-permute-start(f32[3,16,1024]{2,1,0:T(8,128)S(1)} %get-tuple-element.23), channel_id=1, source_target_pairs={{0,4},{4,8},{8,12},{12,16},{16,20},{20,24},{24,28},{28,32},{32,36}... | collective-permute-start | bytes 589832 | tf_op jit(solution)/shard_map/ppermute | solution.py:289
  18.9 8.6 %collective-permute-start.2 = (f32[3,16,1024]{2,1,0:T(8,128)S(1)}, f32[3,16,1024]{2,1,0:T(8,128)S(1)}, u32[]{:S(2)}, u32[]{:S(2)}) collective-permute-start(f32[3,16,1024]{2,1,0:T(8,128)S(1)} %bitcast.24), channel_id=1, source_target_pairs={{0,1},{1,2},{2,3},{3,0},{4,5},{5,6},{6,7},{7,4},{8,9},{9,10},{10,1... | collective-permute-start | bytes 589832 | tf_op jit(solution)/shard_map/ppermute | solution.py:291
  20.4 7.2 %collective-permute-start.3 = (f32[3,16,1024]{2,1,0:T(8,128)S(1)}, f32[3,16,1024]{2,1,0:T(8,128)S(1)}, u32[]{:S(2)}, u32[]{:S(2)}) collective-permute-start(f32[3,16,1024]{2,1,0:T(8,128)S(1)} %bitcast.25), channel_id=1, source_target_pairs={{0,3},{1,0},{2,1},{3,2},{4,7},{5,4},{6,5},{7,6},{8,11},{9,8},{10,9... | collective-permute-start | bytes 589832 | tf_op jit(solution)/shard_map/ppermute | solution.py:292
  23.2 1.9 %copy-start = (f32[3,16,16,1024]{3,2,1,0:T(8,128)S(1)}, f32[3,16,16,1024]{3,2,1,0:T(8,128)}, u32[]{:S(2)}) copy-start(f32[3,16,16,1024]{3,2,1,0:T(8,128)} %refs_1_.1) | copy-start | bytes 9437188
  34.4 1.7 %copy-start.1 = (f32[3,16,16,1024]{3,2,1,0:T(8,128)}, f32[3,16,16,1024]{3,2,1,0:T(8,128)S(1)}, u32[]{:S(2)}) copy-start(f32[3,16,16,1024]{3,2,1,0:T(8,128)S(1)} %substep.2.start_ref) | copy-start | bytes 9437188
  39.2 9.0 %copy-start.4 = (f32[4,8,256]{2,1,0:T(8,128)}, f32[4,8,256]{2,1,0:T(8,128)S(1)}, u32[]{:S(2)}) copy-start(f32[4,8,256]{2,1,0:T(8,128)S(1)} %get-tuple-element.13.refs_2_) | copy-start | bytes 98308
  39.2 30.5 %collective-permute-start.4 = (f32[3,16,1024]{2,1,0:T(8,128)}, f32[3,16,1024]{2,1,0:T(8,128)S(1)}, u32[]{:S(2)}, u32[]{:S(2)}) collective-permute-start(f32[3,16,1024]{2,1,0:T(8,128)} %get-tuple-element.15), channel_id=1, source_target_pairs={{0,4},{4,8},{8,12},{12,16},{16,20},{20,24},{24,28},{28,32},{32,36}... | collective-permute-start | bytes 589832 | tf_op jit(solution)/shard_map/ppermute | solution.py:289
  40.3 29.3 %collective-permute-start.5 = (f32[3,16,1024]{2,1,0:T(8,128)}, f32[3,16,1024]{2,1,0:T(8,128)S(1)}, u32[]{:S(2)}, u32[]{:S(2)}) collective-permute-start(f32[3,16,1024]{2,1,0:T(8,128)} %get-tuple-element.16), channel_id=1, source_target_pairs={{0,124},{4,0},{8,4},{12,8},{16,12},{20,16},{24,20},{28,24},{32,28}... | collective-permute-start | bytes 589832 | tf_op jit(solution)/shard_map/ppermute | solution.py:290
  43.9 25.7 %collective-permute-start.6 = (f32[3,16,1024]{2,1,0:T(8,128)}, f32[3,16,1024]{2,1,0:T(8,128)}, u32[]{:S(2)}, u32[]{:S(2)}) collective-permute-start(f32[3,16,1024]{2,1,0:T(8,128)} %get-tuple-element.17), channel_id=1, source_target_pairs={{0,1},{1,2},{2,3},{3,0},{4,5},{5,6},{6,7},{7,4},{8,9},{9,10},{10,1... | collective-permute-start | bytes 589832 | tf_op jit(solution)/shard_map/ppermute | solution.py:291
  46.7 22.9 %collective-permute-start.7 = (f32[3,16,1024]{2,1,0:T(8,128)}, f32[3,16,1024]{2,1,0:T(8,128)}, u32[]{:S(2)}, u32[]{:S(2)}) collective-permute-start(f32[3,16,1024]{2,1,0:T(8,128)} %get-tuple-element.18), channel_id=1, source_target_pairs={{0,3},{1,0},{2,1},{3,2},{4,7},{5,4},{6,5},{7,6},{8,11},{9,8},{10,9... | collective-permute-start | bytes 589832 | tf_op jit(solution)/shard_map/ppermute | solution.py:292
  69.7 0.8 copy-start.5

commit v2 on v1

v2 whole, which is shorter than its diff:
```python
import functools
import math

import jax
import jax.numpy as jnp
from jax import lax
from jax.experimental import pallas as pl
from jax.experimental.pallas import tpu as pltpu
from jax.sharding import PartitionSpec as P

AXES = ("gx", "gy")
HOST_MAX = 4
BOX = 4
LANES = 256
UNROLL = 14
FIELDS = 8

gauss_norm = math.pi ** (-1.5)
time_step = 0.5
viscosity = 0.15
HIGH = lax.Precision.HIGHEST

VMEM = pl.BlockSpec(memory_space=pltpu.VMEM)
SMEM = pl.BlockSpec(memory_space=pltpu.SMEM)
HBM = pl.BlockSpec(memory_space=pltpu.HBM)
PARAMS = pltpu.CompilerParams(vmem_limit_bytes=24 * 2**20)


def log2(value):
    bits = value.bit_length() - 1
    assert 1 << bits == value
    return bits


def gaussians(points, first_i, first_j, first_z, valid):
    cell_z = lax.broadcasted_iota(jnp.int32, (128, LANES), 0) + first_z
    delta_z = cell_z.astype(jnp.float32) - points[2:3]
    along_z = jnp.where(valid, gauss_norm * jnp.exp(-(delta_z * delta_z)), 0.0)
    tile = lax.broadcasted_iota(jnp.int32, (BOX * BOX, LANES), 0)
    delta_x = (lax.shift_right_logical(tile, 2) + first_i).astype(jnp.float32) - points[0:1]
    delta_y = ((tile & 3) + first_j).astype(jnp.float32) - points[1:2]
    across = jnp.exp(-(delta_x * delta_x + delta_y * delta_y))
    return along_z, across


def valid_lanes(odd, points_n):
    lane = lax.broadcasted_iota(jnp.int32, (1, LANES), 1)
    first = odd * (LANES - points_n)
    return (lane >= first) & (lane < first + points_n)


def rotor_at(info_ref, h):
    return [info_ref[h * FIELDS + f] for f in range(FIELDS)]


def reduce_tiles(product, across, k):
    rows = product[k * BOX * BOX : (k + 1) * BOX * BOX]
    return jnp.sum(rows * across, axis=0, keepdims=True)


def sample_kernel(
    rotors, cx_n, cy_n, tiles_z, full_y, points_n, n_gy,
    meta_ref, points_ref, motion_ref, velocity_ref, cotangent_ref,
    info_ref, terms_ref,
    seen_ref, point_ref, move_ref, block_ref, cell_ref, sems,
):
    log_t, log_y = log2(tiles_z), log2(full_y)
    log_cx, log_cy = log2(cx_n), log2(cy_n)
    gx, gy = meta_ref[2 * rotors], meta_ref[2 * rotors + 1]

    def clear(d, carry):
        seen_ref[d] = 0
        return carry

    lax.fori_loop(0, seen_ref.shape[0], clear, 0, unroll=16)

    def visit(r, count):
        tile = meta_ref[r]
        i = lax.shift_right_logical(tile, log_t + log_y)
        j = lax.shift_right_logical(tile, log_t) & (full_y - 1)
        mine = (lax.shift_right_logical(i, log_cx) == gx) & (lax.shift_right_logical(j, log_cy) == gy)
        own = meta_ref[rotors + r]
        earlier = seen_ref[own]
        seen_ref[own] = earlier + 1

        @pl.when(mine)
        def _():
            base = count * FIELDS
            info_ref[base] = r
            info_ref[base + 1] = i
            info_ref[base + 2] = j
            info_ref[base + 3] = tile & (tiles_z - 1)
            info_ref[base + 4] = own
            info_ref[base + 5] = earlier

        return count + mine.astype(jnp.int32)

    count = lax.fori_loop(0, rotors, visit, jnp.int32(0), unroll=8)
    info_ref[HOST_MAX * FIELDS] = count

    def copies(h):
        r, i, _, kz, _, _, _, _ = rotor_at(info_ref, h)
        start = lax.shift_right_logical(r, 1) * (2 * points_n) + (r & 1) * 128
        lanes = pl.ds(pl.multiple_of(start, 128), LANES)
        cells = pl.ds(pl.multiple_of(kz * 128, 128), 128)
        planes = pl.ds(i & (cx_n - 1), BOX)
        return [
            pltpu.make_async_copy(points_ref.at[:, lanes], point_ref.at[h], sems.at[h, 0]),
            pltpu.make_async_copy(motion_ref.at[:, lanes], move_ref.at[h], sems.at[h, 1]),
            pltpu.make_async_copy(velocity_ref.at[:, planes, :, cells], block_ref.at[h, 0], sems.at[h, 2]),
            pltpu.make_async_copy(cotangent_ref.at[:, planes, :, cells], block_ref.at[h, 1], sems.at[h, 3]),
        ]

    for h in range(HOST_MAX):

        @pl.when(h < count)
        def _(h=h):
            for copy in copies(h):
                copy.start()

    for h in range(HOST_MAX):

        @pl.when(h < count)
        def _(h=h):
            for copy in copies(h):
                copy.wait()
            r, i, j, kz, _, _, _, _ = rotor_at(info_ref, h)
            points, move = point_ref[h], move_ref[h]
            along_z, across = gaussians(points, i, j, kz * 128, valid_lanes(r & 1, points_n))
            rows = pl.ds(j & (cy_n - 1), BOX)
            for field in range(2):
                for k in range(3):
                    for a in range(BOX):
                        at = ((field * 3 + k) * BOX + a) * BOX
                        cell_ref[at : at + BOX, :] = block_ref[h, field, k, a, rows, :]
            product = jnp.dot(cell_ref[...], along_z, precision=HIGH, preferred_element_type=jnp.float32)
            relative = [reduce_tiles(product, across, k) - move[k : k + 1] for k in range(3)]
            speed = jnp.sqrt(sum(v * v for v in relative))
            for k in range(3):
                terms_ref[h, k : k + 1, :] = speed * relative[k]
                terms_ref[h, 3 + k : 4 + k, :] = reduce_tiles(product, across, 3 + k)
                terms_ref[h, 6 + k : 7 + k, :] = points[k : k + 1]
                terms_ref[h, 9 + k : 10 + k, :] = move[k : k + 1]


def spread(along_z, across, force, part_ref, h, j):
    weighted = jnp.concatenate([across * force[k] for k in range(3)], axis=0)
    contrib = lax.dot_general(
        weighted, along_z, (((1,), (1,)), ((), ())), precision=HIGH, preferred_element_type=jnp.float32
    )
    part_ref[h] = jnp.zeros(part_ref.shape[1:], jnp.float32)
    for k in range(3):
        for a in range(BOX):
            at = (k * BOX + a) * BOX
            part_ref[h, k, a, pl.ds(j, BOX)] = time_step * contrib[at : at + BOX]


def add_forces(info_ref, count, part_ref, next_ref, k):
    cx_n = next_ref.shape[1]
    for h in range(HOST_MAX):

        @pl.when(h < count)
        def _(h=h):
            _, i, _, kz, _, _, _, _ = rotor_at(info_ref, h)
            cells = pl.ds(pl.multiple_of(kz * 128, 128), 128)
            where = (k, pl.ds(i & (cx_n - 1), BOX), slice(None), cells)
            next_ref[where] = next_ref[where] + part_ref[h, k]


def laplace(meta_ref, gx_at, n_gx, n_gy, now_ref, halo_refs, next_ref, before, after_each):
    x_low_ref, x_high_ref, y_low_ref, y_high_ref = halo_refs
    _, cx_n, cy_n, cz_n = now_ref.shape
    gx, gy = meta_ref[gx_at], meta_ref[gx_at + 1]
    rate = time_step * viscosity
    subs, tiles = cy_n // 8, cz_n // 128
    row = lax.broadcasted_iota(jnp.int32, (8, 128), 0)
    lane = lax.broadcasted_iota(jnp.int32, (8, 128), 1)
    first_row, last_row, first_lane, last_lane = row == 0, row == 7, lane == 0, lane == 127
    zero = jnp.zeros((8, 128), jnp.float32)

    def flag(condition):
        return jnp.where(condition, 1.0, 0.0).astype(jnp.float32)

    has_x_low, has_x_high = flag(gx > 0), flag(gx < n_gx - 1)
    has_y_low, has_y_high = flag(gy > 0), flag(gy < n_gy - 1)

    def plane(k, x, below, above):
        def at(s, j):
            return now_ref[k, x, s * 8 : s * 8 + 8, j * 128 : j * 128 + 128]

        now = [[at(s, j) for j in range(tiles)] for s in range(subs)]
        for j in range(tiles):
            lanes = slice(j * 128, j * 128 + 128)
            up = [pltpu.roll(now[s][j], 1, 0) for s in range(subs)]
            down = [pltpu.roll(now[s][j], 7, 0) for s in range(subs)]
            low = jnp.broadcast_to(y_low_ref[k, x, :, lanes] * has_y_low, (8, 128))
            high = jnp.broadcast_to(y_high_ref[k, x, :, lanes] * has_y_high, (8, 128))
            for s in range(subs):
                here = now[s][j]
                y_below = jnp.where(first_row, up[s - 1] if s else low, up[s])
                y_above = jnp.where(last_row, down[s + 1] if s < subs - 1 else high, down[s])
                before = pltpu.roll(now[s][j - 1], 1, 1) if j else zero
                after = pltpu.roll(now[s][j + 1], 127, 1) if j < tiles - 1 else zero
                z_below = jnp.where(first_lane, before, pltpu.roll(here, 1, 1))
                z_above = jnp.where(last_lane, after, pltpu.roll(here, 127, 1))
                total = (below(s, j) + above(s, j)) + (y_below + y_above) + (z_below + z_above)
                next_ref[k, x, s * 8 : s * 8 + 8, lanes] = (1.0 - 6.0 * rate) * here + rate * total

    def inside(k, x):
        return lambda s, j: now_ref[k, x, s * 8 : s * 8 + 8, j * 128 : j * 128 + 128]

    def outside(ref, k, scale):
        return lambda s, j: ref[k, s * 8 : s * 8 + 8, j * 128 : j * 128 + 128] * scale

    def component(k, carry):
        before(k)
        plane(k, 0, outside(x_low_ref, k, has_x_low), inside(k, 1))
        plane(k, cx_n - 1, inside(k, cx_n - 2), outside(x_high_ref, k, has_x_high))

        def inner(x, carry):
            plane(k, x, inside(k, x - 1), inside(k, x + 1))
            return carry

        lax.fori_loop(1, cx_n - 1, inner, 0, unroll=UNROLL)
        after_each(k)
        return carry

    lax.fori_loop(0, 3, component, 0)


def aligned(value, rank, odd, points_n):
    earlier = pltpu.roll(value, LANES - points_n, 1)
    later = pltpu.roll(value, points_n, 1)
    return jnp.where(rank == odd, value, jnp.where(rank < odd, earlier, later))


def advance_kernel(
    points_n, gx_at, n_gx, n_gy,
    meta_ref, info_ref, terms_ref, table_ref, field_ref, hx_low_ref, hx_high_ref, hy_low_ref, hy_high_ref,
    out_ref, x_low_ref, x_high_ref, y_low_ref, y_high_ref, send_ref, force_ref,
    now_ref, mid_ref, part_ref, cell_ref, block_ref, sems,
):
    _, cx_n, cy_n, _ = now_ref.shape
    count = info_ref[HOST_MAX * FIELDS]

    def load(k):
        return pltpu.make_async_copy(field_ref.at[k], now_ref.at[k], sems.at[k])

    def save(k):
        return pltpu.make_async_copy(mid_ref.at[k], out_ref.at[k], sems.at[3 + k])

    for k in range(3):
        load(k).start()
    send_ref[...] = jnp.zeros_like(send_ref)

    def setup(h):
        r, i, j, kz, own, rank, _, _ = rotor_at(info_ref, h)
        along_z, across = gaussians(terms_ref[h, 6:9, :], i, j, kz * 128, valid_lanes(r & 1, points_n))
        row = table_ref[own]
        coef = jnp.where(rank > 0, row[:, 128:], row[:, :LANES])
        return along_z, across, (i & (cx_n - 1), j & (cy_n - 1), kz), aligned(coef, rank, r & 1, points_n)

    for h in range(HOST_MAX):

        @pl.when(h < count)
        def _(h=h):
            along_z, across, here, coef = setup(h)
            force = [coef * terms_ref[h, k : k + 1, :] for k in range(3)]
            spread(along_z, across, force, part_ref, h, here[1])

    def after(k):
        add_forces(info_ref, count, part_ref, mid_ref, k)
        save(k).start()

    halo_refs = (hx_low_ref, hx_high_ref, hy_low_ref, hy_high_ref)
    laplace(meta_ref, gx_at, n_gx, n_gy, now_ref, halo_refs, mid_ref, lambda k: load(k).wait(), after)

    for h in range(HOST_MAX):

        @pl.when(h < count)
        def _(h=h):
            along_z, across, (i, j, kz), coef = setup(h)
            r, _, _, _, own, rank, _, _ = rotor_at(info_ref, h)
            block_ref[...] = mid_ref[:, pl.ds(i, BOX), :, pl.ds(pl.multiple_of(kz * 128, 128), 128)]
            for k in range(3):
                for a in range(BOX):
                    at = (k * BOX + a) * BOX
                    cell_ref[at : at + BOX, :] = block_ref[k, a, pl.ds(j, BOX)]
            product = jnp.dot(cell_ref[...], along_z, precision=HIGH, preferred_element_type=jnp.float32)
            relative = [reduce_tiles(product, across, k) - terms_ref[h, 9 + k : 10 + k, :] for k in range(3)]
            speed = jnp.sqrt(sum(v * v for v in relative))
            grad = jnp.zeros((1, LANES), jnp.float32)
            for k in range(3):
                shape_term = speed * relative[k]
                grad = grad + terms_ref[h, 3 + k : 4 + k, :] * shape_term
                force_ref[h, k : k + 1, :] = coef * shape_term
            for k in range(3):
                force_ref[h, 3 + k : 4 + k, :] = terms_ref[h, 6 + k : 7 + k, :]
            grad = aligned(time_step * grad, r & 1, rank, points_n)
            blank = jnp.zeros((1, 128), jnp.float32)
            wide = jnp.where(
                rank > 0, jnp.concatenate([blank, grad], axis=1), jnp.concatenate([grad, blank], axis=1)
            )
            send_ref[own] = send_ref[own] + wide

    for k in range(3):
        write_faces(mid_ref, x_low_ref, x_high_ref, y_low_ref, y_high_ref, k)
    for k in range(3):
        save(k).wait()


def write_faces(field_ref, x_low_ref, x_high_ref, y_low_ref, y_high_ref, k):
    _, cx_n, cy_n, _ = field_ref.shape
    x_low_ref[k] = field_ref[k, 0]
    x_high_ref[k] = field_ref[k, cx_n - 1]
    for x in range(cx_n):
        y_low_ref[k, x] = field_ref[k, x, 0:1]
        y_high_ref[k, x] = field_ref[k, x, cy_n - 1 : cy_n]


def faces_kernel(field_ref, x_low_ref, x_high_ref, y_low_ref, y_high_ref, now_ref, sems):
    def load(k):
        return pltpu.make_async_copy(field_ref.at[k], now_ref.at[k], sems.at[k])

    for k in range(3):
        load(k).start()
    for k in range(3):
        load(k).wait()
        write_faces(now_ref, x_low_ref, x_high_ref, y_low_ref, y_high_ref, k)


def finish_kernel(
    points_n, gx_at, n_gx, n_gy,
    meta_ref, info_ref, force_ref, field_ref, x_low_ref, x_high_ref, y_low_ref, y_high_ref,
    out_ref,
    now_ref, next_ref, part_ref, sems,
):
    _, cx_n, cy_n, _ = now_ref.shape

    def load(k):
        return pltpu.make_async_copy(field_ref.at[k], now_ref.at[k], sems.at[k])

    def save(k):
        return pltpu.make_async_copy(next_ref.at[k], out_ref.at[k], sems.at[3 + k])

    for k in range(3):
        load(k).start()
    count = info_ref[HOST_MAX * FIELDS]
    for h in range(HOST_MAX):

        @pl.when(h < count)
        def _(h=h):
            r, i, j, kz, _, _, _, _ = rotor_at(info_ref, h)
            along_z, across = gaussians(force_ref[h, 3:6, :], i, j, kz * 128, valid_lanes(r & 1, points_n))
            force = [force_ref[h, k : k + 1, :] for k in range(3)]
            spread(along_z, across, force, part_ref, h, j & (cy_n - 1))

    def after(k):
        add_forces(info_ref, count, part_ref, next_ref, k)
        save(k).start()

    halo_refs = (x_low_ref, x_high_ref, y_low_ref, y_high_ref)
    laplace(meta_ref, gx_at, n_gx, n_gy, now_ref, halo_refs, next_ref, lambda k: load(k).wait(), after)
    for k in range(3):
        save(k).wait()


def ring(count, step):
    return [(i, (i + step) % count) for i in range(count)]


def exchange(faces, n_gx, n_gy):
    x_low, x_high, y_low, y_high = faces
    return (
        lax.ppermute(x_high, "gx", ring(n_gx, 1)),
        lax.ppermute(x_low, "gx", ring(n_gx, -1)),
        lax.ppermute(y_high, "gy", ring(n_gy, 1)),
        lax.ppermute(y_low, "gy", ring(n_gy, -1)),
    )


def per_device(velocity, cotangent, points, motion, coef, readers, owner):
    velocity, cotangent, points, motion = (
        pltpu.with_memory_space_constraint(array, pltpu.HBM) for array in (velocity, cotangent, points, motion)
    )
    _, cx_n, cy_n, cz_n = velocity.shape
    tiles_z = cz_n // 128
    n_gx, n_gy = lax.axis_size("gx"), lax.axis_size("gy")
    devices = n_gx * n_gy
    full_y = cy_n * n_gy
    rotors = readers.shape[0]
    points_n = points.shape[1] // rotors
    own_n = coef.shape[0]
    f32 = jnp.float32
    field = pltpu.HBM(velocity.shape, f32)
    face_x = jax.ShapeDtypeStruct((3, cy_n, cz_n), f32)
    face_y = jax.ShapeDtypeStruct((3, cx_n, 1, cz_n), f32)
    faces = (face_x, face_x, face_y, face_y)
    rows = jax.ShapeDtypeStruct((devices, 1, own_n), f32)

    table = lax.all_to_all(jnp.broadcast_to(coef[None, None], (devices, 1, own_n)), AXES, 0, 0, tiled=True)
    meta = jnp.concatenate(
        [readers[:, 0], owner, lax.axis_index("gx")[None], lax.axis_index("gy")[None]]
    ).astype(jnp.int32)
    halos = exchange(
        pl.pallas_call(
            faces_kernel, out_shape=faces, in_specs=[HBM], out_specs=(VMEM,) * 4,
            scratch_shapes=[pltpu.VMEM(velocity.shape, f32), pltpu.SemaphoreType.DMA((3,))],
            compiler_params=PARAMS, name="faces",
        )(velocity),
        n_gx, n_gy,
    )

    info, terms = pl.pallas_call(
        functools.partial(sample_kernel, rotors, cx_n, cy_n, tiles_z, full_y, points_n, n_gy),
        out_shape=(
            jax.ShapeDtypeStruct((64,), jnp.int32),
            jax.ShapeDtypeStruct((HOST_MAX, 16, LANES), f32),
        ),
        in_specs=[SMEM, HBM, HBM, HBM, HBM],
        out_specs=(SMEM, VMEM),
        scratch_shapes=[
            pltpu.SMEM((devices,), jnp.int32),
            pltpu.VMEM((HOST_MAX, 3, LANES), f32),
            pltpu.VMEM((HOST_MAX, 3, LANES), f32),
            pltpu.VMEM((HOST_MAX, 2, 3, BOX, cy_n, 128), f32),
            pltpu.VMEM((6 * BOX * BOX, 128), f32),
            pltpu.SemaphoreType.DMA((HOST_MAX, 4)),
        ],
        compiler_params=PARAMS,
        name="sample",
    )(meta, points, motion, velocity, cotangent)

    mid, *mid_faces, send, force = pl.pallas_call(
        functools.partial(advance_kernel, points_n, 2 * rotors, n_gx, n_gy),
        out_shape=(field, *faces, rows, jax.ShapeDtypeStruct((HOST_MAX, 8, LANES), f32)),
        in_specs=[SMEM, SMEM, VMEM, VMEM, HBM] + [VMEM] * 4,
        out_specs=(HBM,) + (VMEM,) * 6,
        scratch_shapes=[
            pltpu.VMEM(velocity.shape, f32),
            pltpu.VMEM(velocity.shape, f32),
            pltpu.VMEM((HOST_MAX, 3, BOX, cy_n, 128), f32),
            pltpu.VMEM((3 * BOX * BOX, 128), f32),
            pltpu.VMEM((3, BOX, cy_n, 128), f32),
            pltpu.SemaphoreType.DMA((6,)),
        ],
        compiler_params=PARAMS,
        name="advance",
    )(meta, info, terms, table, velocity, *halos)

    received = lax.all_to_all(send, AXES, 0, 0, tiled=True)
    halos = exchange(mid_faces, n_gx, n_gy)
    velocity_out = pl.pallas_call(
        functools.partial(finish_kernel, points_n, 2 * rotors, n_gx, n_gy),
        out_shape=field,
        in_specs=[SMEM, SMEM, VMEM, HBM] + [VMEM] * 4,
        out_specs=HBM,
        scratch_shapes=[
            pltpu.VMEM(velocity.shape, f32),
            pltpu.VMEM(velocity.shape, f32),
            pltpu.VMEM((HOST_MAX, 3, BOX, cy_n, 128), f32),
            pltpu.SemaphoreType.DMA((6,)),
        ],
        compiler_params=PARAMS,
        name="finish",
    )(meta, info, force, pltpu.with_memory_space_constraint(mid, pltpu.HBM), *halos)
    velocity_out, received = lax.optimization_barrier((velocity_out, received))
    return velocity_out, jnp.sum(received, axis=(0, 1))


def solution(mesh):
    cells = P(None, "gx", "gy", None)
    return jax.shard_map(
        per_device,
        mesh=mesh,
        in_specs=(cells, cells, P(), P(), P(AXES), P(), P()),
        out_specs=(cells, P(AXES)),
        check_vma=False,
    )
```

time: 79.5 us -> 57.7 us (0.73); the launches traced: 78.1 us -> 57.5 us
  blocking collectives: 19.8 us -> 0 us
  local copies, waits for them, and re-layouts: 10.1 us -> 2.16 us
  starting transfers between devices: 25 us -> 31.7 us
  waiting for transfers between devices: 0.02 us -> 5.96 us
  Pallas kernels: 20 us -> 16 us
  other arithmetic: 2.41 us -> 0.83 us
    all_to_all x1 -> x0, blocking collectives: 19.8 us -> none  [per_device(): received = lax.all_to_all(send, AXES, 0, 0, tiled=True)]
    all_to_all x1 -> x2, starting transfers between devices: 11.5 us -> 20.3 us  [the longest x1 11.5 us: per_device(): lax.all_to_all(jnp.broadcast_to(coef[None, None], (devices, 1, own_n)), A...]
    all_to_all x1 -> x2, waiting for transfers between devices: 0.01 us -> 5.94 us  [the longest x1 5.93 us: per_device(): received = lax.all_to_all(send, AXES, 0, 0, tiled=True)]
    pallas_call x3, Pallas kernels: 17.7 us -> 12.2 us  [the longest x1 5.46 us: per_device(): pl.pallas_call(functools.partial(advance_kernel, points_n, 2 * rotors, n_...]
    unnamed x15 -> x2, local copies, waits for them, and re-layouts: 4.4 us -> 0.01 us
    ppermute x2, starting transfers between devices: 4.77 us -> 1.65 us  [exchange(): lax.ppermute(x_low, 'gx', ring(n_gx, -1))]
    ppermute x2, starting transfers between devices: 1.87 us -> 4.33 us  [exchange(): lax.ppermute(x_high, 'gx', ring(n_gx, 1))]
    slice x1 -> x0, local copies, waits for them, and re-layouts: 2.26 us -> none  [per_device(): velocity[:, :, 0]]
  transfers between devices with their start and end apart: 9 -> 10, of which waited for: 0 -> 1; matrix products, arithmetic and copies ran while one was open for 9% -> 1% of each run, Pallas kernels for 3% -> 18%
where the time goes in v2:
time: 57.7 us; the launch traced here: 57.5 us
  starting transfers between devices  31.7 us (55%)
  Pallas kernels  16 us (28%)
  waiting for transfers between devices  5.96 us (10%)
  local copies, waits for them, and re-layouts  2.16 us (4%)
  other arithmetic  0.83 us (1%)
  between operations  0.76 us (1%)
    all_to_all x1, starting transfers between devices, per_device(): lax.all_to_all(jnp.broadcast_to(coef[None, None], (devices, 1, own_n)), A...  11.5 us
    all_to_all x1, starting transfers between devices, per_device(): received = lax.all_to_all(send, AXES, 0, 0, tiled=True)  8.75 us
    all_to_all x1, waiting for transfers between devices, per_device(): received = lax.all_to_all(send, AXES, 0, 0, tiled=True)  5.93 us
    pallas_call x1, Pallas kernels, per_device(): pl.pallas_call(functools.partial(advance_kernel, points_n, 2 * rotors, n_...  5.46 us
    pallas_call x1, Pallas kernels, per_device(): pl.pallas_call(functools.partial(finish_kernel, points_n, 2 * rotors, n_g...  4.78 us
    ppermute x2, starting transfers between devices, exchange(): lax.ppermute(x_high, 'gx', ring(n_gx, 1))  4.33 us
    pallas_call x1, Pallas kernels, per_device(): pl.pallas_call(functools.partial(sample_kernel, rotors, cx_n, cy_n, tiles...  3.87 us
    ppermute x2, starting transfers between devices, exchange(): lax.ppermute(y_low, 'gy', ring(n_gy, -1))  3.08 us
  transfers between devices with their start and end apart: 10, of which 1 were waited for; matrix products, arithmetic and copies ran while one was open for 1% of the time, Pallas kernels for 18%

profile of v2, /device:TPU:1, one launch (start us, length us, event | category | flops | bytes accessed | tf_op | source)
XLA Modules:
  0.0 57.5 jit_solution(4004281591293463222)
XLA Ops:
  0.6 0.0 copy-start
  0.6 1.5 %broadcast_in_dim.14 = f32[128,1,384]{2,1,0:T(1,128)} broadcast(f32[384]{0:T(512)} %param.11), dimensions={2} | broadcast | bytes 198144 | tf_op jit(solution)/shard_map/broadcast_in_dim | solution.py:401
  2.1 11.5 %all-to-all-start = ((f32[128,1,384]{2,1,0:T(1,128)}), f32[128,1,384]{2,1,0:T(1,128)S(1)}, u32[]{:S(2)}, u32[]{:S(2)}) async-start(f32[128,1,384]{2,1,0:T(1,128)} %broadcast_in_dim.14), calls=%async_computation | async-start | bytes 393216 | tf_op jit(solution)/shard_map/all_to_all | solution.py:401
  13.6 1.9 %faces.1 = (f32[3,16,1024]{2,1,0:T(8,128)S(1)}, f32[3,16,1024]{2,1,0:T(8,128)S(1)}, f32[3,16,1,1024]{3,2,1,0:T(1,128)S(1)}, f32[3,16,1,1024]{3,2,1,0:T(1,128)S(1)}) custom-call(f32[3,16,16,1024]{3,2,1,0:T(8,128)} %field_ref.3), custom_call_target="tpu_custom_call" | custom-call | tf_op jit(solution)/shard_map/faces/pallas_call | solution.py:406
  15.5 1.8 %collective-permute-start = (f32[3,16,1024]{2,1,0:T(8,128)S(1)}, f32[3,16,1024]{2,1,0:T(8,128)S(1)}, u32[]{:S(2)}, u32[]{:S(2)}) collective-permute-start(f32[3,16,1024]{2,1,0:T(8,128)S(1)} %get-tuple-element.19), channel_id=1, source_target_pairs={{0,4},{4,8},{8,12},{12,16},{16,20},{20,24},{24,28},{28,32},{32,36}... | collective-permute-start | bytes 589832 | tf_op jit(solution)/shard_map/ppermute | solution.py:375
  17.4 0.0 collective-permute-start.1
  17.4 1.2 %collective-permute-start.2 = (f32[3,16,1,1024]{3,2,1,0:T(1,128)S(1)}, f32[3,16,1,1024]{3,2,1,0:T(1,128)S(1)}, u32[]{:S(2)}, u32[]{:S(2)}) collective-permute-start(f32[3,16,1,1024]{3,2,1,0:T(1,128)S(1)} %get-tuple-element.21), channel_id=1, source_target_pairs={{0,1},{1,2},{2,3},{3,0},{4,5},{5,6},{6,7},{7,4},{8,9},{9,10},{10,1... | collective-permute-start | bytes 589832 | tf_op jit(solution)/shard_map/ppermute | solution.py:377
  18.6 1.5 %collective-permute-start.3 = (f32[3,16,1,1024]{3,2,1,0:T(1,128)S(1)}, f32[3,16,1,1024]{3,2,1,0:T(1,128)S(1)}, u32[]{:S(2)}, u32[]{:S(2)}) collective-permute-start(f32[3,16,1,1024]{3,2,1,0:T(1,128)S(1)} %get-tuple-element.22), channel_id=1, source_target_pairs={{0,3},{1,0},{2,1},{3,2},{4,7},{5,4},{6,5},{7,6},{8,11},{9,8},{10,9... | collective-permute-start | bytes 589832 | tf_op jit(solution)/shard_map/ppermute | solution.py:378
  20.0 0.7 %slice_bitcast_fusion = s32[96]{0:T(128)S(1)} fusion(s32[96,16]{0,1:T(8,128)} %param.12), kind=kLoop, calls=%fused_computation.1 | loop fusion | bytes 768 | tf_op jit(solution)/shard_map/squeeze | solution.py:403
  20.7 0.0 copy-done
  20.7 0.1 pad_add_fusion.meta_ref
  20.8 3.9 %sample.1 = (s32[64]{0:T(128)S(1)}, f32[4,16,256]{2,1,0:T(8,128)S(1)}) custom-call(s32[194]{0:T(256)S(1)} %pad_add_fusion.meta_ref, f32[3,18432]{1,0:T(4,128)} %points_ref.1, f32[3,18432]{1,0:T(4,128)} %motion_ref.1, f32[3,16,16,1024]{3,2,1,0:T(8,128)} %field_ref.3, f32[3,16,16,1024]{3,2,1,0:T(8,128)} %cotangent_ref.1), custom_call_target="tpu_custom_call" | custom-call | tf_op jit(solution)/shard_map/sample/pallas_call | solution.py:414
  24.7 0.0 all-to-all-done.table_ref
  24.7 0.0 collective-permute-done.hx_low_ref
  24.7 0.0 collective-permute-done.1.hx_high_ref
  24.7 0.0 collective-permute-done.2.hy_low_ref
  24.7 0.0 collective-permute-done.3.hy_high_ref
  24.7 5.5 %advance.1 = (f32[3,16,16,1024]{3,2,1,0:T(8,128)}, f32[3,16,1024]{2,1,0:T(8,128)S(1)}, f32[3,16,1024]{2,1,0:T(8,128)S(1)}, f32[3,16,1,1024]{3,2,1,0:T(1,128)S(1)...) custom-call(s32[194]{0:T(256)S(1)} %pad_add_fusion.meta_ref, ...), custom_call_target="tpu_custom_call" | custom-call | tf_op jit(solution)/shard_map/advance/pallas_call | solution.py:434
  30.2 2.5 %collective-permute-start.4 = (f32[3,16,1024]{2,1,0:T(8,128)S(1)}, f32[3,16,1024]{2,1,0:T(8,128)S(1)}, u32[]{:S(2)}, u32[]{:S(2)}) collective-permute-start(f32[3,16,1024]{2,1,0:T(8,128)S(1)} %get-tuple-element.25), channel_id=1, source_target_pairs={{0,4},{4,8},{8,12},{12,16},{16,20},{20,24},{24,28},{28,32},{32,36}... | collective-permute-start | bytes 589832 | tf_op jit(solution)/shard_map/ppermute | solution.py:375
  32.7 1.7 %collective-permute-start.5 = (f32[3,16,1024]{2,1,0:T(8,128)S(1)}, f32[3,16,1024]{2,1,0:T(8,128)S(1)}, u32[]{:S(2)}, u32[]{:S(2)}) collective-permute-start(f32[3,16,1024]{2,1,0:T(8,128)S(1)} %get-tuple-element.26), channel_id=1, source_target_pairs={{0,124},{4,0},{8,4},{12,8},{16,12},{20,16},{24,20},{28,24},{32,28}... | collective-permute-start | bytes 589832 | tf_op jit(solution)/shard_map/ppermute | solution.py:376
  34.4 1.2 %collective-permute-start.6 = (f32[3,16,1,1024]{3,2,1,0:T(1,128)S(1)}, f32[3,16,1,1024]{3,2,1,0:T(1,128)S(1)}, u32[]{:S(2)}, u32[]{:S(2)}) collective-permute-start(f32[3,16,1,1024]{3,2,1,0:T(1,128)S(1)} %get-tuple-element.27), channel_id=1, source_target_pairs={{0,1},{1,2},{2,3},{3,0},{4,5},{5,6},{6,7},{7,4},{8,9},{9,10},{10,1... | collective-permute-start | bytes 589832 | tf_op jit(solution)/shard_map/ppermute | solution.py:377
  35.6 1.6 %collective-permute-start.7 = (f32[3,16,1,1024]{3,2,1,0:T(1,128)S(1)}, f32[3,16,1,1024]{3,2,1,0:T(1,128)S(1)}, u32[]{:S(2)}, u32[]{:S(2)}) collective-permute-start(f32[3,16,1,1024]{3,2,1,0:T(1,128)S(1)} %get-tuple-element.28), channel_id=1, source_target_pairs={{0,3},{1,0},{2,1},{3,2},{4,7},{5,4},{6,5},{7,6},{8,11},{9,8},{10,9... | collective-permute-start | bytes 589832 | tf_op jit(solution)/shard_map/ppermute | solution.py:378
  37.2 8.8 %all-to-all-start.1 = ((f32[128,1,384]{2,1,0:T(1,128)}), f32[128,1,384]{2,1,0:T(1,128)S(1)}, u32[]{:S(2)}, u32[]{:S(2)}) async-start(f32[128,1,384]{2,1,0:T(1,128)} %get-tuple-element.29), calls=%async_computation.1 | async-start | bytes 393216 | tf_op jit(solution)/shard_map/all_to_all | solution.py:451
  46.0 0.0 collective-permute-done.4.x_low_ref
  46.0 0.0 collective-permute-done.5.x_high_ref
  46.0 0.0 collective-permute-done.6.y_low_ref
  46.0 0.0 collective-permute-done.7.y_high_ref
  46.0 4.8 %finish.1 = f32[3,16,16,1024]{3,2,1,0:T(8,128)} custom-call(s32[194]{0:T(256)S(1)} %pad_add_fusion.meta_ref, s32[64]{0:T(128)S(1)} %get-tuple-element.17.info_ref, f32[4,8,256]{2,1,0:T(8,128)S(1)} %get-tuple-element.23.force_ref, f32[3,16,16,1024]{3,2,1,0:T(8,128)} %get-tuple-element.24.field_ref, f32[3,16,1024]{2,1,0:T(8,128)S(1)} %collective-permute-done.4.x_low_ref, ...), custom_call_target="tpu_custom_call" | custom-call | tf_op jit(solution)/shard_map/finish/pallas_call | solution.py:453
  50.8 5.9 %all-to-all-done.1 = f32[128,1,384]{2,1,0:T(1,128)S(1)} async-done(((f32[128,1,384]{2,1,0:T(1,128)}), f32[128,1,384]{2,1,0:T(1,128)S(1)}, u32[]{:S(2)}, u32[]{:S(2)}) %all-to-all-start.1) | async-done | bytes 196640 | tf_op jit(solution)/shard_map/all_to_all | solution.py:451
  56.7 0.8 %reduce_sum.9 = f32[384]{0:T(512)} reduce(f32[128,1,384]{2,1,0:T(1,128)S(1)} %all-to-all-done.1, f32[]{:T(128)} %constant.10.clone.1), dimensions={0,1}, to_apply=%region_0.0 | reduce | flops 48768 | bytes 198148 | tf_op jit(solution)/shard_map/reduce_sum | solution.py:468
Async XLA Ops:
  0.6 20.1 %copy-start = (s32[96]{0:T(128)S(1)}, s32[96]{0:T(128)}, u32[]{:S(2)}) copy-start(s32[96]{0:T(128)} %param.13) | copy-start | bytes 1156
  2.1 22.6 %all-to-all-start = ((f32[128,1,384]{2,1,0:T(1,128)}), f32[128,1,384]{2,1,0:T(1,128)S(1)}, u32[]{:S(2)}, u32[]{:S(2)}) async-start(f32[128,1,384]{2,1,0:T(1,128)} %broadcast_in_dim.14), calls=%async_computation | async-start | bytes 393216 | tf_op jit(solution)/shard_map/all_to_all | solution.py:401
  15.5 9.2 %collective-permute-start = (f32[3,16,1024]{2,1,0:T(8,128)S(1)}, f32[3,16,1024]{2,1,0:T(8,128)S(1)}, u32[]{:S(2)}, u32[]{:S(2)}) collective-permute-start(f32[3,16,1024]{2,1,0:T(8,128)S(1)} %get-tuple-element.19), channel_id=1, source_target_pairs={{0,4},{4,8},{8,12},{12,16},{16,20},{20,24},{24,28},{28,32},{32,36}... | collective-permute-start | bytes 589832 | tf_op jit(solution)/shard_map/ppermute | solution.py:375
  17.4 7.3 %collective-permute-start.1 = (f32[3,16,1024]{2,1,0:T(8,128)S(1)}, f32[3,16,1024]{2,1,0:T(8,128)S(1)}, u32[]{:S(2)}, u32[]{:S(2)}) collective-permute-start(f32[3,16,1024]{2,1,0:T(8,128)S(1)} %get-tuple-element.20), channel_id=1, source_target_pairs={{0,124},{4,0},{8,4},{12,8},{16,12},{20,16},{24,20},{28,24},{32,28}... | collective-permute-start | bytes 589832 | tf_op jit(solution)/shard_map/ppermute | solution.py:376
  17.4 7.4 %collective-permute-start.2 = (f32[3,16,1,1024]{3,2,1,0:T(1,128)S(1)}, f32[3,16,1,1024]{3,2,1,0:T(1,128)S(1)}, u32[]{:S(2)}, u32[]{:S(2)}) collective-permute-start(f32[3,16,1,1024]{3,2,1,0:T(1,128)S(1)} %get-tuple-element.21), channel_id=1, source_target_pairs={{0,1},{1,2},{2,3},{3,0},{4,5},{5,6},{6,7},{7,4},{8,9},{9,10},{10,1... | collective-permute-start | bytes 589832 | tf_op jit(solution)/shard_map/ppermute | solution.py:377
  18.6 6.2 %collective-permute-start.3 = (f32[3,16,1,1024]{3,2,1,0:T(1,128)S(1)}, f32[3,16,1,1024]{3,2,1,0:T(1,128)S(1)}, u32[]{:S(2)}, u32[]{:S(2)}) collective-permute-start(f32[3,16,1,1024]{3,2,1,0:T(1,128)S(1)} %get-tuple-element.22), channel_id=1, source_target_pairs={{0,3},{1,0},{2,1},{3,2},{4,7},{5,4},{6,5},{7,6},{8,11},{9,8},{10,9... | collective-permute-start | bytes 589832 | tf_op jit(solution)/shard_map/ppermute | solution.py:378
  30.2 15.8 %collective-permute-start.4 = (f32[3,16,1024]{2,1,0:T(8,128)S(1)}, f32[3,16,1024]{2,1,0:T(8,128)S(1)}, u32[]{:S(2)}, u32[]{:S(2)}) collective-permute-start(f32[3,16,1024]{2,1,0:T(8,128)S(1)} %get-tuple-element.25), channel_id=1, source_target_pairs={{0,4},{4,8},{8,12},{12,16},{16,20},{20,24},{24,28},{28,32},{32,36}... | collective-permute-start | bytes 589832 | tf_op jit(solution)/shard_map/ppermute | solution.py:375
  32.7 13.3 %collective-permute-start.5 = (f32[3,16,1024]{2,1,0:T(8,128)S(1)}, f32[3,16,1024]{2,1,0:T(8,128)S(1)}, u32[]{:S(2)}, u32[]{:S(2)}) collective-permute-start(f32[3,16,1024]{2,1,0:T(8,128)S(1)} %get-tuple-element.26), channel_id=1, source_target_pairs={{0,124},{4,0},{8,4},{12,8},{16,12},{20,16},{24,20},{28,24},{32,28}... | collective-permute-start | bytes 589832 | tf_op jit(solution)/shard_map/ppermute | solution.py:376
  34.4 11.6 %collective-permute-start.6 = (f32[3,16,1,1024]{3,2,1,0:T(1,128)S(1)}, f32[3,16,1,1024]{3,2,1,0:T(1,128)S(1)}, u32[]{:S(2)}, u32[]{:S(2)}) collective-permute-start(f32[3,16,1,1024]{3,2,1,0:T(1,128)S(1)} %get-tuple-element.27), channel_id=1, source_target_pairs={{0,1},{1,2},{2,3},{3,0},{4,5},{5,6},{6,7},{7,4},{8,9},{9,10},{10,1... | collective-permute-start | bytes 589832 | tf_op jit(solution)/shard_map/ppermute | solution.py:377
  35.6 10.4 %collective-permute-start.7 = (f32[3,16,1,1024]{3,2,1,0:T(1,128)S(1)}, f32[3,16,1,1024]{3,2,1,0:T(1,128)S(1)}, u32[]{:S(2)}, u32[]{:S(2)}) collective-permute-start(f32[3,16,1,1024]{3,2,1,0:T(1,128)S(1)} %get-tuple-element.28), channel_id=1, source_target_pairs={{0,3},{1,0},{2,1},{3,2},{4,7},{5,4},{6,5},{7,6},{8,11},{9,8},{10,9... | collective-permute-start | bytes 589832 | tf_op jit(solution)/shard_map/ppermute | solution.py:378
  37.2 19.5 %all-to-all-start.1 = ((f32[128,1,384]{2,1,0:T(1,128)}), f32[128,1,384]{2,1,0:T(1,128)S(1)}, u32[]{:S(2)}, u32[]{:S(2)}) async-start(f32[128,1,384]{2,1,0:T(1,128)} %get-tuple-element.29), calls=%async_computation.1 | async-start | bytes 393216 | tf_op jit(solution)/shard_map/all_to_all | solution.py:451

commit v3 on v2

--- a/solution.py
+++ b/solution.py
@@ -237,8 +237,8 @@
 def advance_kernel(
     points_n, gx_at, n_gx, n_gy,
     meta_ref, info_ref, terms_ref, table_ref, field_ref, hx_low_ref, hx_high_ref, hy_low_ref, hy_high_ref,
-    out_ref, x_low_ref, x_high_ref, y_low_ref, y_high_ref, send_ref, force_ref,
-    now_ref, mid_ref, part_ref, cell_ref, block_ref, sems,
+    out_ref, x_low_ref, x_high_ref, y_low_ref, y_high_ref, rows_ref, force_ref,
+    now_ref, mid_ref, part_ref, cell_ref, block_ref, send_ref, sems,
 ):
     _, cx_n, cy_n, _ = now_ref.shape
     count = info_ref[HOST_MAX * FIELDS]
@@ -303,8 +303,11 @@
             )
             send_ref[own] = send_ref[own] + wide
 
+    store = pltpu.make_async_copy(send_ref, rows_ref, sems.at[6])
+    store.start()
     for k in range(3):
         write_faces(mid_ref, x_low_ref, x_high_ref, y_low_ref, y_high_ref, k)
+    store.wait()
     for k in range(3):
         save(k).wait()
 
@@ -318,15 +321,24 @@
         y_high_ref[k, x] = field_ref[k, x, cy_n - 1 : cy_n]
 
 
-def faces_kernel(field_ref, x_low_ref, x_high_ref, y_low_ref, y_high_ref, now_ref, sems):
+def faces_kernel(
+    coef_ref, field_ref, out_ref, x_low_ref, x_high_ref, y_low_ref, y_high_ref, row_ref, table_ref, now_ref, sems
+):
     def load(k):
         return pltpu.make_async_copy(field_ref.at[k], now_ref.at[k], sems.at[k])
 
+    fetch = pltpu.make_async_copy(coef_ref, row_ref, sems.at[3])
+    fetch.start()
     for k in range(3):
         load(k).start()
+    fetch.wait()
+    table_ref[...] = jnp.broadcast_to(row_ref[...].reshape(1, 1, row_ref.shape[0]), table_ref.shape)
+    store = pltpu.make_async_copy(table_ref, out_ref, sems.at[4])
+    store.start()
     for k in range(3):
         load(k).wait()
         write_faces(now_ref, x_low_ref, x_high_ref, y_low_ref, y_high_ref, k)
+    store.wait()
 
 
 def finish_kernel(
@@ -396,20 +408,27 @@
     face_x = jax.ShapeDtypeStruct((3, cy_n, cz_n), f32)
     face_y = jax.ShapeDtypeStruct((3, cx_n, 1, cz_n), f32)
     faces = (face_x, face_x, face_y, face_y)
-    rows = jax.ShapeDtypeStruct((devices, 1, own_n), f32)
-
-    table = lax.all_to_all(jnp.broadcast_to(coef[None, None], (devices, 1, own_n)), AXES, 0, 0, tiled=True)
+    rows = pltpu.HBM((devices, 1, own_n), f32)
+
     meta = jnp.concatenate(
         [readers[:, 0], owner, lax.axis_index("gx")[None], lax.axis_index("gy")[None]]
     ).astype(jnp.int32)
-    halos = exchange(
-        pl.pallas_call(
-            faces_kernel, out_shape=faces, in_specs=[HBM], out_specs=(VMEM,) * 4,
-            scratch_shapes=[pltpu.VMEM(velocity.shape, f32), pltpu.SemaphoreType.DMA((3,))],
-            compiler_params=PARAMS, name="faces",
-        )(velocity),
-        n_gx, n_gy,
-    )
+    table, *first_faces = pl.pallas_call(
+        faces_kernel,
+        out_shape=(rows, *faces),
+        in_specs=[HBM, HBM],
+        out_specs=(HBM,) + (VMEM,) * 4,
+        scratch_shapes=[
+            pltpu.VMEM((own_n,), f32),
+            pltpu.VMEM((devices, 1, own_n), f32),
+            pltpu.VMEM(velocity.shape, f32),
+            pltpu.SemaphoreType.DMA((5,)),
+        ],
+        compiler_params=PARAMS,
+        name="faces",
+    )(pltpu.with_memory_space_constraint(coef, pltpu.HBM), velocity)
+    table = lax.all_to_all(table, AXES, 0, 0, tiled=True)
+    halos = exchange(first_faces, n_gx, n_gy)
 
     info, terms = pl.pallas_call(
         functools.partial(sample_kernel, rotors, cx_n, cy_n, tiles_z, full_y, points_n, n_gy),
@@ -428,6 +447,7 @@
             pltpu.SemaphoreType.DMA((HOST_MAX, 4)),
         ],
         compiler_params=PARAMS,
+        cost_estimate=pl.CostEstimate(flops=2**33, transcendentals=0, bytes_accessed=2**26),
         name="sample",
     )(meta, points, motion, velocity, cotangent)
 
@@ -435,14 +455,15 @@
         functools.partial(advance_kernel, points_n, 2 * rotors, n_gx, n_gy),
         out_shape=(field, *faces, rows, jax.ShapeDtypeStruct((HOST_MAX, 8, LANES), f32)),
         in_specs=[SMEM, SMEM, VMEM, VMEM, HBM] + [VMEM] * 4,
-        out_specs=(HBM,) + (VMEM,) * 6,
+        out_specs=(HBM,) + (VMEM,) * 4 + (HBM, VMEM),
         scratch_shapes=[
             pltpu.VMEM(velocity.shape, f32),
             pltpu.VMEM(velocity.shape, f32),
             pltpu.VMEM((HOST_MAX, 3, BOX, cy_n, 128), f32),
             pltpu.VMEM((3 * BOX * BOX, 128), f32),
             pltpu.VMEM((3, BOX, cy_n, 128), f32),
-            pltpu.SemaphoreType.DMA((6,)),
+            pltpu.VMEM((devices, 1, own_n), f32),
+            pltpu.SemaphoreType.DMA((7,)),
         ],
         compiler_params=PARAMS,
         name="advance",

time: 57.7 us -> 56.2 us (0.974)
  local copies, waits for them, and re-layouts: 2.16 us -> 0.69 us
  waiting for transfers between devices: 5.96 us -> 7.4 us
  starting transfers between devices: 31.7 us -> 30.6 us
    ppermute x2, starting transfers between devices: 4.33 us -> 2.56 us  [exchange(): lax.ppermute(x_high, 'gx', ring(n_gx, 1))]
    all_to_all x1, waiting for transfers between devices: 0.01 us -> 1.48 us  [per_device(): table = lax.all_to_all(table, AXES, 0, 0, tiled=True)]
    broadcast_in_dim x1 -> x0, local copies, waits for them, and re-layouts: 1.47 us -> none  [per_device(): jnp.broadcast_to(coef[None, None], (devices, 1, own_n))]
    ppermute x2, starting transfers between devices: 2.42 us -> 1.8 us  [exchange(): lax.ppermute(y_high, 'gy', ring(n_gy, 1))]
    ppermute x2, starting transfers between devices: 1.65 us -> 2.24 us  [exchange(): lax.ppermute(x_low, 'gx', ring(n_gx, -1))]
  transfers between devices with their start and end apart: 10 -> 10, of which waited for: 1 -> 2; matrix products, arithmetic and copies ran while one was open for 1% -> 1% of each run, Pallas kernels for 18% -> 15%
where the time goes in v3:
time: 56.2 us
  starting transfers between devices  30.6 us (54%)
  Pallas kernels  15.9 us (28%)
  waiting for transfers between devices  7.4 us (13%)
  other arithmetic  0.83 us (1%)
  between operations  0.74 us (1%)
  local copies, waits for them, and re-layouts  0.69 us (1%)
    all_to_all x1, starting transfers between devices, per_device(): table = lax.all_to_all(table, AXES, 0, 0, tiled=True)  11.5 us
    all_to_all x1, starting transfers between devices, per_device(): received = lax.all_to_all(send, AXES, 0, 0, tiled=True)  8.9 us
    all_to_all x1, waiting for transfers between devices, per_device(): received = lax.all_to_all(send, AXES, 0, 0, tiled=True)  5.9 us
    pallas_call x1, Pallas kernels, per_device(): pl.pallas_call(functools.partial(advance_kernel, points_n, 2 * rotors, n_...  5.24 us
    pallas_call x1, Pallas kernels, per_device(): pl.pallas_call(functools.partial(finish_kernel, points_n, 2 * rotors, n_g...  4.81 us
    pallas_call x1, Pallas kernels, per_device(): pl.pallas_call(functools.partial(sample_kernel, rotors, cx_n, cy_n, tiles...  3.87 us
    ppermute x2, starting transfers between devices, exchange(): lax.ppermute(y_low, 'gy', ring(n_gy, -1))  3.55 us
    ppermute x2, starting transfers between devices, exchange(): lax.ppermute(x_high, 'gx', ring(n_gx, 1))  2.56 us
  transfers between devices with their start and end apart: 10, of which 2 were waited for; matrix products, arithmetic and copies ran while one was open for 1% of the time, Pallas kernels for 15%

profile of v3, /device:TPU:1, one launch (start us, length us, event | category | flops | bytes accessed | tf_op | source)
XLA Modules:
  0.0 56.2 jit_solution(4782448325395923251)
XLA Ops:
  0.6 0.0 copy-start
  0.6 2.0 %faces.1 = (f32[128,1,384]{2,1,0:T(1,128)}, f32[3,16,1024]{2,1,0:T(8,128)S(1)}, f32[3,16,1024]{2,1,0:T(8,128)S(1)}, f32[3,16,1,1024]{3,2,1,0:T(1,128)S(1)}, f32[3,16,1,1024]{3,2,1,0:T(1,128)S(1)}) custom-call(f32[384]{0:T(512)} %coef_ref.1, f32[3,16,16,1024]{3,2,1,0:T(8,128)} %field_ref.3), custom_call_target="tpu_custom_call" | custom-call | tf_op jit(solution)/shard_map/faces/pallas_call | solution.py:416
  2.7 11.5 %all-to-all-start = ((f32[128,1,384]{2,1,0:T(1,128)}), f32[128,1,384]{2,1,0:T(1,128)S(1)}, u32[]{:S(2)}, u32[]{:S(2)}) async-start(f32[128,1,384]{2,1,0:T(1,128)} %get-tuple-element.20), calls=%async_computation | async-start | bytes 393216 | tf_op jit(solution)/shard_map/all_to_all | solution.py:430
  14.2 1.8 %collective-permute-start = (f32[3,16,1024]{2,1,0:T(8,128)S(1)}, f32[3,16,1024]{2,1,0:T(8,128)S(1)}, u32[]{:S(2)}, u32[]{:S(2)}) collective-permute-start(f32[3,16,1024]{2,1,0:T(8,128)S(1)} %get-tuple-element.21), channel_id=1, source_target_pairs={{0,4},{4,8},{8,12},{12,16},{16,20},{20,24},{24,28},{28,32},{32,36}... | collective-permute-start | bytes 589832 | tf_op jit(solution)/shard_map/ppermute | solution.py:387
  16.0 0.0 collective-permute-start.1
  16.0 1.2 %collective-permute-start.2 = (f32[3,16,1,1024]{3,2,1,0:T(1,128)S(1)}, f32[3,16,1,1024]{3,2,1,0:T(1,128)S(1)}, u32[]{:S(2)}, u32[]{:S(2)}) collective-permute-start(f32[3,16,1,1024]{3,2,1,0:T(1,128)S(1)} %get-tuple-element.23), channel_id=1, source_target_pairs={{0,1},{1,2},{2,3},{3,0},{4,5},{5,6},{6,7},{7,4},{8,9},{9,10},{10,1... | collective-permute-start | bytes 589832 | tf_op jit(solution)/shard_map/ppermute | solution.py:389
  17.2 1.5 %collective-permute-start.3 = (f32[3,16,1,1024]{3,2,1,0:T(1,128)S(1)}, f32[3,16,1,1024]{3,2,1,0:T(1,128)S(1)}, u32[]{:S(2)}, u32[]{:S(2)}) collective-permute-start(f32[3,16,1,1024]{3,2,1,0:T(1,128)S(1)} %get-tuple-element.24), channel_id=1, source_target_pairs={{0,3},{1,0},{2,1},{3,2},{4,7},{5,4},{6,5},{7,6},{8,11},{9,8},{10,9... | collective-permute-start | bytes 589832 | tf_op jit(solution)/shard_map/ppermute | solution.py:390
  18.7 0.7 %slice_bitcast_fusion = s32[96]{0:T(128)S(1)} fusion(s32[96,16]{0,1:T(8,128)} %param.12), kind=kLoop, calls=%fused_computation.1 | loop fusion | bytes 768 | tf_op jit(solution)/shard_map/squeeze | solution.py:414
  19.4 0.0 copy-done
  19.4 0.1 pad_add_fusion.meta_ref
  19.5 3.9 %sample.1 = (s32[64]{0:T(128)S(1)}, f32[4,16,256]{2,1,0:T(8,128)S(1)}) custom-call(s32[194]{0:T(256)S(1)} %pad_add_fusion.meta_ref, f32[3,18432]{1,0:T(4,128)} %points_ref.1, f32[3,18432]{1,0:T(4,128)} %motion_ref.1, f32[3,16,16,1024]{3,2,1,0:T(8,128)} %field_ref.3, f32[3,16,16,1024]{3,2,1,0:T(8,128)} %cotangent_ref.1), custom_call_target="tpu_custom_call" | custom-call | flops 8589934592 | bytes 67108864 | tf_op jit(solution)/shard_map/sample/pallas_call | solution.py:433
  23.3 1.5 %all-to-all-done.table_ref = f32[128,1,384]{2,1,0:T(1,128)S(1)} async-done(((f32[128,1,384]{2,1,0:T(1,128)}), f32[128,1,384]{2,1,0:T(1,128)S(1)}, u32[]{:S(2)}, u32[]{:S(2)}) %all-to-all-start) | async-done | bytes 196640 | tf_op jit(solution)/shard_map/all_to_all | solution.py:430
  24.8 0.0 collective-permute-done.hx_low_ref
  24.8 0.0 collective-permute-done.1.hx_high_ref
  24.8 0.0 collective-permute-done.2.hy_low_ref
  24.8 0.0 collective-permute-done.3.hy_high_ref
  24.8 5.2 %advance.1 = (f32[3,16,16,1024]{3,2,1,0:T(8,128)}, f32[3,16,1024]{2,1,0:T(8,128)S(1)}, f32[3,16,1024]{2,1,0:T(8,128)S(1)}, f32[3,16,1,1024]{3,2,1,0:T(1,128)S(1)...) custom-call(s32[194]{0:T(256)S(1)} %pad_add_fusion.meta_ref, ...), custom_call_target="tpu_custom_call" | custom-call | tf_op jit(solution)/shard_map/advance/pallas_call | solution.py:454
  30.1 0.7 %collective-permute-start.4 = (f32[3,16,1024]{2,1,0:T(8,128)S(1)}, f32[3,16,1024]{2,1,0:T(8,128)S(1)}, u32[]{:S(2)}, u32[]{:S(2)}) collective-permute-start(f32[3,16,1024]{2,1,0:T(8,128)S(1)} %get-tuple-element.27), channel_id=1, source_target_pairs={{0,4},{4,8},{8,12},{12,16},{16,20},{20,24},{24,28},{28,32},{32,36}... | collective-permute-start | bytes 589832 | tf_op jit(solution)/shard_map/ppermute | solution.py:387
  30.8 2.2 %collective-permute-start.5 = (f32[3,16,1024]{2,1,0:T(8,128)S(1)}, f32[3,16,1024]{2,1,0:T(8,128)S(1)}, u32[]{:S(2)}, u32[]{:S(2)}) collective-permute-start(f32[3,16,1024]{2,1,0:T(8,128)S(1)} %get-tuple-element.28), channel_id=1, source_target_pairs={{0,124},{4,0},{8,4},{12,8},{16,12},{20,16},{24,20},{28,24},{32,28}... | collective-permute-start | bytes 589832 | tf_op jit(solution)/shard_map/ppermute | solution.py:388
  33.1 0.6 %collective-permute-start.6 = (f32[3,16,1,1024]{3,2,1,0:T(1,128)S(1)}, f32[3,16,1,1024]{3,2,1,0:T(1,128)S(1)}, u32[]{:S(2)}, u32[]{:S(2)}) collective-permute-start(f32[3,16,1,1024]{3,2,1,0:T(1,128)S(1)} %get-tuple-element.29), channel_id=1, source_target_pairs={{0,1},{1,2},{2,3},{3,0},{4,5},{5,6},{6,7},{7,4},{8,9},{9,10},{10,1... | collective-permute-start | bytes 589832 | tf_op jit(solution)/shard_map/ppermute | solution.py:389
  33.7 2.1 %collective-permute-start.7 = (f32[3,16,1,1024]{3,2,1,0:T(1,128)S(1)}, f32[3,16,1,1024]{3,2,1,0:T(1,128)S(1)}, u32[]{:S(2)}, u32[]{:S(2)}) collective-permute-start(f32[3,16,1,1024]{3,2,1,0:T(1,128)S(1)} %get-tuple-element.30), channel_id=1, source_target_pairs={{0,3},{1,0},{2,1},{3,2},{4,7},{5,4},{6,5},{7,6},{8,11},{9,8},{10,9... | collective-permute-start | bytes 589832 | tf_op jit(solution)/shard_map/ppermute | solution.py:390
  35.7 8.9 %all-to-all-start.1 = ((f32[128,1,384]{2,1,0:T(1,128)}), f32[128,1,384]{2,1,0:T(1,128)S(1)}, u32[]{:S(2)}, u32[]{:S(2)}) async-start(f32[128,1,384]{2,1,0:T(1,128)} %get-tuple-element.31), calls=%async_computation.1 | async-start | bytes 393216 | tf_op jit(solution)/shard_map/all_to_all | solution.py:472
  44.6 0.0 collective-permute-done.4.x_low_ref
  44.7 0.0 collective-permute-done.5.x_high_ref
  44.7 0.0 collective-permute-done.6.y_low_ref
  44.7 0.0 collective-permute-done.7.y_high_ref
  44.7 4.8 %finish.1 = f32[3,16,16,1024]{3,2,1,0:T(8,128)} custom-call(s32[194]{0:T(256)S(1)} %pad_add_fusion.meta_ref, s32[64]{0:T(128)S(1)} %get-tuple-element.18.info_ref, f32[4,8,256]{2,1,0:T(8,128)S(1)} %get-tuple-element.25.force_ref, f32[3,16,16,1024]{3,2,1,0:T(8,128)} %get-tuple-element.26.field_ref, f32[3,16,1024]{2,1,0:T(8,128)S(1)} %collective-permute-done.4.x_low_ref, ...), custom_call_target="tpu_custom_call" | custom-call | tf_op jit(solution)/shard_map/finish/pallas_call | solution.py:474
  49.5 5.9 %all-to-all-done.1 = f32[128,1,384]{2,1,0:T(1,128)S(1)} async-done(((f32[128,1,384]{2,1,0:T(1,128)}), f32[128,1,384]{2,1,0:T(1,128)S(1)}, u32[]{:S(2)}, u32[]{:S(2)}) %all-to-all-start.1) | async-done | bytes 196640 | tf_op jit(solution)/shard_map/all_to_all | solution.py:472
  55.4 0.8 %reduce_sum.9 = f32[384]{0:T(512)} reduce(f32[128,1,384]{2,1,0:T(1,128)S(1)} %all-to-all-done.1, f32[]{:T(128)} %constant.10.clone.1), dimensions={0,1}, to_apply=%region_0.0 | reduce | flops 48768 | bytes 198148 | tf_op jit(solution)/shard_map/reduce_sum | solution.py:489
Async XLA Ops:
  0.6 18.7 %copy-start = (s32[96]{0:T(128)S(1)}, s32[96]{0:T(128)}, u32[]{:S(2)}) copy-start(s32[96]{0:T(128)} %param.13) | copy-start | bytes 1156
  2.7 22.1 %all-to-all-start = ((f32[128,1,384]{2,1,0:T(1,128)}), f32[128,1,384]{2,1,0:T(1,128)S(1)}, u32[]{:S(2)}, u32[]{:S(2)}) async-start(f32[128,1,384]{2,1,0:T(1,128)} %get-tuple-element.20), calls=%async_computation | async-start | bytes 393216 | tf_op jit(solution)/shard_map/all_to_all | solution.py:430
  14.2 10.6 %collective-permute-start = (f32[3,16,1024]{2,1,0:T(8,128)S(1)}, f32[3,16,1024]{2,1,0:T(8,128)S(1)}, u32[]{:S(2)}, u32[]{:S(2)}) collective-permute-start(f32[3,16,1024]{2,1,0:T(8,128)S(1)} %get-tuple-element.21), channel_id=1, source_target_pairs={{0,4},{4,8},{8,12},{12,16},{16,20},{20,24},{24,28},{28,32},{32,36}... | collective-permute-start | bytes 589832 | tf_op jit(solution)/shard_map/ppermute | solution.py:387
  16.0 8.8 %collective-permute-start.1 = (f32[3,16,1024]{2,1,0:T(8,128)S(1)}, f32[3,16,1024]{2,1,0:T(8,128)S(1)}, u32[]{:S(2)}, u32[]{:S(2)}) collective-permute-start(f32[3,16,1024]{2,1,0:T(8,128)S(1)} %get-tuple-element.22), channel_id=1, source_target_pairs={{0,124},{4,0},{8,4},{12,8},{16,12},{20,16},{24,20},{28,24},{32,28}... | collective-permute-start | bytes 589832 | tf_op jit(solution)/shard_map/ppermute | solution.py:388
  16.0 8.8 %collective-permute-start.2 = (f32[3,16,1,1024]{3,2,1,0:T(1,128)S(1)}, f32[3,16,1,1024]{3,2,1,0:T(1,128)S(1)}, u32[]{:S(2)}, u32[]{:S(2)}) collective-permute-start(f32[3,16,1,1024]{3,2,1,0:T(1,128)S(1)} %get-tuple-element.23), channel_id=1, source_target_pairs={{0,1},{1,2},{2,3},{3,0},{4,5},{5,6},{6,7},{7,4},{8,9},{9,10},{10,1... | collective-permute-start | bytes 589832 | tf_op jit(solution)/shard_map/ppermute | solution.py:389
  17.2 7.6 %collective-permute-start.3 = (f32[3,16,1,1024]{3,2,1,0:T(1,128)S(1)}, f32[3,16,1,1024]{3,2,1,0:T(1,128)S(1)}, u32[]{:S(2)}, u32[]{:S(2)}) collective-permute-start(f32[3,16,1,1024]{3,2,1,0:T(1,128)S(1)} %get-tuple-element.24), channel_id=1, source_target_pairs={{0,3},{1,0},{2,1},{3,2},{4,7},{5,4},{6,5},{7,6},{8,11},{9,8},{10,9... | collective-permute-start | bytes 589832 | tf_op jit(solution)/shard_map/ppermute | solution.py:390
  30.1 14.6 %collective-permute-start.4 = (f32[3,16,1024]{2,1,0:T(8,128)S(1)}, f32[3,16,1024]{2,1,0:T(8,128)S(1)}, u32[]{:S(2)}, u32[]{:S(2)}) collective-permute-start(f32[3,16,1024]{2,1,0:T(8,128)S(1)} %get-tuple-element.27), channel_id=1, source_target_pairs={{0,4},{4,8},{8,12},{12,16},{16,20},{20,24},{24,28},{28,32},{32,36}... | collective-permute-start | bytes 589832 | tf_op jit(solution)/shard_map/ppermute | solution.py:387
  30.8 13.8 %collective-permute-start.5 = (f32[3,16,1024]{2,1,0:T(8,128)S(1)}, f32[3,16,1024]{2,1,0:T(8,128)S(1)}, u32[]{:S(2)}, u32[]{:S(2)}) collective-permute-start(f32[3,16,1024]{2,1,0:T(8,128)S(1)} %get-tuple-element.28), channel_id=1, source_target_pairs={{0,124},{4,0},{8,4},{12,8},{16,12},{20,16},{24,20},{28,24},{32,28}... | collective-permute-start | bytes 589832 | tf_op jit(solution)/shard_map/ppermute | solution.py:388
  33.1 11.6 %collective-permute-start.6 = (f32[3,16,1,1024]{3,2,1,0:T(1,128)S(1)}, f32[3,16,1,1024]{3,2,1,0:T(1,128)S(1)}, u32[]{:S(2)}, u32[]{:S(2)}) collective-permute-start(f32[3,16,1,1024]{3,2,1,0:T(1,128)S(1)} %get-tuple-element.29), channel_id=1, source_target_pairs={{0,1},{1,2},{2,3},{3,0},{4,5},{5,6},{6,7},{7,4},{8,9},{9,10},{10,1... | collective-permute-start | bytes 589832 | tf_op jit(solution)/shard_map/ppermute | solution.py:389
  33.7 11.0 %collective-permute-start.7 = (f32[3,16,1,1024]{3,2,1,0:T(1,128)S(1)}, f32[3,16,1,1024]{3,2,1,0:T(1,128)S(1)}, u32[]{:S(2)}, u32[]{:S(2)}) collective-permute-start(f32[3,16,1,1024]{3,2,1,0:T(1,128)S(1)} %get-tuple-element.30), channel_id=1, source_target_pairs={{0,3},{1,0},{2,1},{3,2},{4,7},{5,4},{6,5},{7,6},{8,11},{9,8},{10,9... | collective-permute-start | bytes 589832 | tf_op jit(solution)/shard_map/ppermute | solution.py:390
  35.7 19.7 %all-to-all-start.1 = ((f32[128,1,384]{2,1,0:T(1,128)}), f32[128,1,384]{2,1,0:T(1,128)S(1)}, u32[]{:S(2)}, u32[]{:S(2)}) async-start(f32[128,1,384]{2,1,0:T(1,128)} %get-tuple-element.31), calls=%async_computation.1 | async-start | bytes 393216 | tf_op jit(solution)/shard_map/all_to_all | solution.py:472

commit v4 on v3

--- a/solution.py
+++ b/solution.py
@@ -58,45 +58,47 @@
     return jnp.sum(rows * across, axis=0, keepdims=True)
 
 
-def sample_kernel(
-    rotors, cx_n, cy_n, tiles_z, full_y, points_n, n_gy,
-    meta_ref, points_ref, motion_ref, velocity_ref, cotangent_ref,
-    info_ref, terms_ref,
-    seen_ref, point_ref, move_ref, block_ref, cell_ref, sems,
-):
+def search(rotors, cx_n, cy_n, tiles_z, full_y, at_ref, tiles_ref, owner_ref, owners_ref, info_ref, found_ref):
     log_t, log_y = log2(tiles_z), log2(full_y)
     log_cx, log_cy = log2(cx_n), log2(cy_n)
-    gx, gy = meta_ref[2 * rotors], meta_ref[2 * rotors + 1]
-
-    def clear(d, carry):
-        seen_ref[d] = 0
-        return carry
-
-    lax.fori_loop(0, seen_ref.shape[0], clear, 0, unroll=16)
+    gx, gy = at_ref[0], at_ref[1]
+    for h in range(HOST_MAX + 1):
+        found_ref[h] = 0
 
     def visit(r, count):
-        tile = meta_ref[r]
-        i = lax.shift_right_logical(tile, log_t + log_y)
-        j = lax.shift_right_logical(tile, log_t) & (full_y - 1)
-        mine = (lax.shift_right_logical(i, log_cx) == gx) & (lax.shift_right_logical(j, log_cy) == gy)
-        own = meta_ref[rotors + r]
-        earlier = seen_ref[own]
-        seen_ref[own] = earlier + 1
-
-        @pl.when(mine)
-        def _():
-            base = count * FIELDS
-            info_ref[base] = r
-            info_ref[base + 1] = i
-            info_ref[base + 2] = j
-            info_ref[base + 3] = tile & (tiles_z - 1)
-            info_ref[base + 4] = own
-            info_ref[base + 5] = earlier
-
-        return count + mine.astype(jnp.int32)
-
-    count = lax.fori_loop(0, rotors, visit, jnp.int32(0), unroll=8)
+        tile = tiles_ref[0, r]
+        x = lax.shift_right_logical(tile, log_t + log_y + log_cx)
+        y = lax.shift_right_logical(tile, log_t + log_cy) & ((full_y >> log_cy) - 1)
+        found_ref[count] = r
+        return count + ((x == gx) & (y == gy)).astype(jnp.int32)
+
+    count = lax.fori_loop(0, rotors, visit, jnp.int32(0), unroll=16)
     info_ref[HOST_MAX * FIELDS] = count
+    owners = owners_ref[...]
+    lane = lax.broadcasted_iota(jnp.int32, owners.shape, 1)
+    chosen = [found_ref[h] for h in range(HOST_MAX)]
+    earlier = [jnp.sum(jnp.where((owners == owner_ref[r]) & (lane < r), 1.0, 0.0)) for r in chosen]
+    for h, r in enumerate(chosen):
+        tile = tiles_ref[0, r]
+        base = h * FIELDS
+        info_ref[base] = r
+        info_ref[base + 1] = lax.shift_right_logical(tile, log_t + log_y)
+        info_ref[base + 2] = lax.shift_right_logical(tile, log_t) & (full_y - 1)
+        info_ref[base + 3] = tile & (tiles_z - 1)
+        info_ref[base + 4] = owner_ref[r]
+        info_ref[base + 5] = earlier[h].astype(jnp.int32)
+        info_ref[base + 6] = 0
+        info_ref[base + 7] = 0
+
+
+def sample_kernel(
+    rotors, cx_n, cy_n, tiles_z, full_y, points_n,
+    at_ref, owner_ref, owners_ref, tiles_ref, points_ref, motion_ref, velocity_ref, cotangent_ref,
+    info_ref, terms_ref,
+    found_ref, point_ref, move_ref, block_ref, cell_ref, sems,
+):
+    search(rotors, cx_n, cy_n, tiles_z, full_y, at_ref, tiles_ref, owner_ref, owners_ref, info_ref, found_ref)
+    count = info_ref[HOST_MAX * FIELDS]
 
     def copies(h):
         r, i, _, kz, _, _, _, _ = rotor_at(info_ref, h)
@@ -167,10 +169,10 @@
             next_ref[where] = next_ref[where] + part_ref[h, k]
 
 
-def laplace(meta_ref, gx_at, n_gx, n_gy, now_ref, halo_refs, next_ref, before, after_each):
+def laplace(at_ref, n_gx, n_gy, now_ref, halo_refs, next_ref, before, after_each):
     x_low_ref, x_high_ref, y_low_ref, y_high_ref = halo_refs
     _, cx_n, cy_n, cz_n = now_ref.shape
-    gx, gy = meta_ref[gx_at], meta_ref[gx_at + 1]
+    gx, gy = at_ref[0], at_ref[1]
     rate = time_step * viscosity
     subs, tiles = cy_n // 8, cz_n // 128
     row = lax.broadcasted_iota(jnp.int32, (8, 128), 0)
@@ -225,7 +227,8 @@
         after_each(k)
         return carry
 
-    lax.fori_loop(0, 3, component, 0)
+    for k in range(3):
+        component(k, 0)
 
 
 def aligned(value, rank, odd, points_n):
@@ -235,8 +238,8 @@
 
 
 def advance_kernel(
-    points_n, gx_at, n_gx, n_gy,
-    meta_ref, info_ref, terms_ref, table_ref, field_ref, hx_low_ref, hx_high_ref, hy_low_ref, hy_high_ref,
+    points_n, n_gx, n_gy,
+    at_ref, info_ref, terms_ref, table_ref, field_ref, hx_low_ref, hx_high_ref, hy_low_ref, hy_high_ref,
     out_ref, x_low_ref, x_high_ref, y_low_ref, y_high_ref, rows_ref, force_ref,
     now_ref, mid_ref, part_ref, cell_ref, block_ref, send_ref, sems,
 ):
@@ -273,7 +276,7 @@
         save(k).start()
 
     halo_refs = (hx_low_ref, hx_high_ref, hy_low_ref, hy_high_ref)
-    laplace(meta_ref, gx_at, n_gx, n_gy, now_ref, halo_refs, mid_ref, lambda k: load(k).wait(), after)
+    laplace(at_ref, n_gx, n_gy, now_ref, halo_refs, mid_ref, lambda k: load(k).wait(), after)
 
     for h in range(HOST_MAX):
 
@@ -342,8 +345,8 @@
 
 
 def finish_kernel(
-    points_n, gx_at, n_gx, n_gy,
-    meta_ref, info_ref, force_ref, field_ref, x_low_ref, x_high_ref, y_low_ref, y_high_ref,
+    points_n, n_gx, n_gy,
+    at_ref, info_ref, force_ref, field_ref, x_low_ref, x_high_ref, y_low_ref, y_high_ref,
     out_ref,
     now_ref, next_ref, part_ref, sems,
 ):
@@ -372,7 +375,7 @@
         save(k).start()
 
     halo_refs = (x_low_ref, x_high_ref, y_low_ref, y_high_ref)
-    laplace(meta_ref, gx_at, n_gx, n_gy, now_ref, halo_refs, next_ref, lambda k: load(k).wait(), after)
+    laplace(at_ref, n_gx, n_gy, now_ref, halo_refs, next_ref, lambda k: load(k).wait(), after)
     for k in range(3):
         save(k).wait()
 
@@ -410,9 +413,7 @@
     faces = (face_x, face_x, face_y, face_y)
     rows = pltpu.HBM((devices, 1, own_n), f32)
 
-    meta = jnp.concatenate(
-        [readers[:, 0], owner, lax.axis_index("gx")[None], lax.axis_index("gy")[None]]
-    ).astype(jnp.int32)
+    at = jnp.stack([lax.axis_index("gx"), lax.axis_index("gy")]).astype(jnp.int32)
     table, *first_faces = pl.pallas_call(
         faces_kernel,
         out_shape=(rows, *faces),
@@ -431,15 +432,15 @@
     halos = exchange(first_faces, n_gx, n_gy)
 
     info, terms = pl.pallas_call(
-        functools.partial(sample_kernel, rotors, cx_n, cy_n, tiles_z, full_y, points_n, n_gy),
+        functools.partial(sample_kernel, rotors, cx_n, cy_n, tiles_z, full_y, points_n),
         out_shape=(
             jax.ShapeDtypeStruct((64,), jnp.int32),
             jax.ShapeDtypeStruct((HOST_MAX, 16, LANES), f32),
         ),
-        in_specs=[SMEM, HBM, HBM, HBM, HBM],
+        in_specs=[SMEM, SMEM, VMEM, SMEM] + [HBM] * 4,
         out_specs=(SMEM, VMEM),
         scratch_shapes=[
-            pltpu.SMEM((devices,), jnp.int32),
+            pltpu.SMEM((HOST_MAX + 1,), jnp.int32),
             pltpu.VMEM((HOST_MAX, 3, LANES), f32),
             pltpu.VMEM((HOST_MAX, 3, LANES), f32),
             pltpu.VMEM((HOST_MAX, 2, 3, BOX, cy_n, 128), f32),
@@ -449,10 +450,10 @@
         compiler_params=PARAMS,
         cost_estimate=pl.CostEstimate(flops=2**33, transcendentals=0, bytes_accessed=2**26),
         name="sample",
-    )(meta, points, motion, velocity, cotangent)
+    )(at, owner, owner.reshape(1, rotors), readers.T, points, motion, velocity, cotangent)
 
     mid, *mid_faces, send, force = pl.pallas_call(
-        functools.partial(advance_kernel, points_n, 2 * rotors, n_gx, n_gy),
+        functools.partial(advance_kernel, points_n, n_gx, n_gy),
         out_shape=(field, *faces, rows, jax.ShapeDtypeStruct((HOST_MAX, 8, LANES), f32)),
         in_specs=[SMEM, SMEM, VMEM, VMEM, HBM] + [VMEM] * 4,
         out_specs=(HBM,) + (VMEM,) * 4 + (HBM, VMEM),
@@ -467,12 +468,12 @@
         ],
         compiler_params=PARAMS,
         name="advance",
-    )(meta, info, terms, table, velocity, *halos)
+    )(at, info, terms, table, velocity, *halos)
 
     received = lax.all_to_all(send, AXES, 0, 0, tiled=True)
     halos = exchange(mid_faces, n_gx, n_gy)
     velocity_out = pl.pallas_call(
-        functools.partial(finish_kernel, points_n, 2 * rotors, n_gx, n_gy),
+        functools.partial(finish_kernel, points_n, n_gx, n_gy),
         out_shape=field,
         in_specs=[SMEM, SMEM, VMEM, HBM] + [VMEM] * 4,
         out_specs=HBM,
@@ -484,7 +485,7 @@
         ],
         compiler_params=PARAMS,
         name="finish",
-    )(meta, info, force, pltpu.with_memory_space_constraint(mid, pltpu.HBM), *halos)
+    )(at, info, force, pltpu.with_memory_space_constraint(mid, pltpu.HBM), *halos)
     velocity_out, received = lax.optimization_barrier((velocity_out, received))
     return velocity_out, jnp.sum(received, axis=(0, 1))
 

time: 56.2 us -> 55.8 us (level)
  waiting for transfers between devices: 7.4 us -> 8.8 us
  Pallas kernels: 15.9 us -> 14.9 us
  local copies, waits for them, and re-layouts: 0.69 us -> 0.01 us
    all_to_all x1, waiting for transfers between devices: 1.48 us -> 2.85 us  [per_device(): table = lax.all_to_all(table, AXES, 0, 0, tiled=True)]
    squeeze x1 -> x0, local copies, waits for them, and re-layouts: 0.69 us -> none  [per_device(): readers[:, 0]]
    pallas_call x1, Pallas kernels: 3.87 us -> 3.19 us  [per_device(): pl.pallas_call(functools.partial(sample_kernel, rotors, cx_n, cy_n, tiles...]
    ppermute x2, starting transfers between devices: 1.8 us -> 2.4 us  [exchange(): lax.ppermute(y_high, 'gy', ring(n_gy, 1))]
    ppermute x2, starting transfers between devices: 2.24 us -> 1.65 us  [exchange(): lax.ppermute(x_low, 'gx', ring(n_gx, -1))]
  transfers between devices with their start and end apart: 10 -> 10, of which waited for: 2 -> 2; matrix products, arithmetic and copies ran while one was open for 1% -> 0% of each run, Pallas kernels for 15% -> 14%
where the time goes in v4:
time: 55.8 us; the launch traced here: 55.6 us
  starting transfers between devices  30.4 us (54%)
  Pallas kernels  14.9 us (27%)
  waiting for transfers between devices  8.8 us (16%)
  other arithmetic  0.83 us (1%)
  between operations  0.74 us (1%)
    all_to_all x1, starting transfers between devices, per_device(): table = lax.all_to_all(table, AXES, 0, 0, tiled=True)  11.5 us
    all_to_all x1, starting transfers between devices, per_device(): received = lax.all_to_all(send, AXES, 0, 0, tiled=True)  8.82 us
    all_to_all x1, waiting for transfers between devices, per_device(): received = lax.all_to_all(send, AXES, 0, 0, tiled=True)  5.93 us
    pallas_call x1, Pallas kernels, per_device(): pl.pallas_call(functools.partial(advance_kernel, points_n, n_gx, n_gy), o...  4.87 us
    pallas_call x1, Pallas kernels, per_device(): pl.pallas_call(functools.partial(finish_kernel, points_n, n_gx, n_gy), ou...  4.79 us
    pallas_call x1, Pallas kernels, per_device(): pl.pallas_call(functools.partial(sample_kernel, rotors, cx_n, cy_n, tiles...  3.19 us
    ppermute x2, starting transfers between devices, exchange(): lax.ppermute(y_low, 'gy', ring(n_gy, -1))  3.06 us
    ppermute x2, starting transfers between devices, exchange(): lax.ppermute(x_high, 'gx', ring(n_gx, 1))  2.93 us
  transfers between devices with their start and end apart: 10, of which 2 were waited for; matrix products, arithmetic and copies ran while one was open for 0% of the time, Pallas kernels for 14%

profile of v4, /device:TPU:1, one launch (start us, length us, event | category | flops | bytes accessed | tf_op | source)
XLA Modules:
  0.0 55.6 jit_solution(14952493542468120909)
XLA Ops:
  0.6 0.0 copy-start.1
  0.6 0.0 copy-start
  0.7 2.0 %faces.1 = (f32[128,1,384]{2,1,0:T(1,128)}, f32[3,16,1024]{2,1,0:T(8,128)S(1)}, f32[3,16,1024]{2,1,0:T(8,128)S(1)}, f32[3,16,1,1024]{3,2,1,0:T(1,128)S(1)}, f32[3,16,1,1024]{3,2,1,0:T(1,128)S(1)}) custom-call(f32[384]{0:T(512)} %coef_ref.1, f32[3,16,16,1024]{3,2,1,0:T(8,128)} %field_ref.3), custom_call_target="tpu_custom_call" | custom-call | tf_op jit(solution)/shard_map/faces/pallas_call | solution.py:417
  2.7 11.5 %all-to-all-start = ((f32[128,1,384]{2,1,0:T(1,128)}), f32[128,1,384]{2,1,0:T(1,128)S(1)}, u32[]{:S(2)}, u32[]{:S(2)}) async-start(f32[128,1,384]{2,1,0:T(1,128)} %get-tuple-element.20), calls=%async_computation | async-start | bytes 393216 | tf_op jit(solution)/shard_map/all_to_all | solution.py:431
  14.2 1.8 %collective-permute-start = (f32[3,16,1024]{2,1,0:T(8,128)S(1)}, f32[3,16,1024]{2,1,0:T(8,128)S(1)}, u32[]{:S(2)}, u32[]{:S(2)}) collective-permute-start(f32[3,16,1024]{2,1,0:T(8,128)S(1)} %get-tuple-element.21), channel_id=1, source_target_pairs={{0,4},{4,8},{8,12},{12,16},{16,20},{20,24},{24,28},{28,32},{32,36}... | collective-permute-start | bytes 589832 | tf_op jit(solution)/shard_map/ppermute | solution.py:390
  16.0 0.0 collective-permute-start.1
  16.0 1.2 %collective-permute-start.2 = (f32[3,16,1,1024]{3,2,1,0:T(1,128)S(1)}, f32[3,16,1,1024]{3,2,1,0:T(1,128)S(1)}, u32[]{:S(2)}, u32[]{:S(2)}) collective-permute-start(f32[3,16,1,1024]{3,2,1,0:T(1,128)S(1)} %get-tuple-element.23), channel_id=1, source_target_pairs={{0,1},{1,2},{2,3},{3,0},{4,5},{5,6},{6,7},{7,4},{8,9},{9,10},{10,1... | collective-permute-start | bytes 589832 | tf_op jit(solution)/shard_map/ppermute | solution.py:392
  17.2 1.5 %collective-permute-start.3 = (f32[3,16,1,1024]{3,2,1,0:T(1,128)S(1)}, f32[3,16,1,1024]{3,2,1,0:T(1,128)S(1)}, u32[]{:S(2)}, u32[]{:S(2)}) collective-permute-start(f32[3,16,1,1024]{3,2,1,0:T(1,128)S(1)} %get-tuple-element.24), channel_id=1, source_target_pairs={{0,3},{1,0},{2,1},{3,2},{4,7},{5,4},{6,5},{7,6},{8,11},{9,8},{10,9... | collective-permute-start | bytes 589832 | tf_op jit(solution)/shard_map/ppermute | solution.py:393
  18.7 0.1 pad_add_fusion.at_ref
  18.8 0.0 copy-done.1
  18.8 0.0 copy-done
  18.8 3.2 %sample.1 = (s32[64]{0:T(128)S(1)}, f32[4,16,256]{2,1,0:T(8,128)S(1)}) custom-call(s32[2]{0:T(128)S(1)} %pad_add_fusion.at_ref, s32[96]{0:T(128)S(1)} %copy-done.1, s32[1,96]{1,0:T(1,128)S(1)} %bitcast.5, s32[16,96]{1,0:T(8,128)S(1)} %bitcast.4, f32[3,18432]{1,0:T(4,128)} %points_ref.1, f32[3,18432]{1,0:T(4,128)} %motion_ref.1, ...), custom_call_target="tpu_custom_call" | custom-call | flops 8589934592 | bytes 67108864 | tf_op jit(solution)/shard_map/sample/pallas_call | solution.py:434
  22.0 2.9 %all-to-all-done.table_ref = f32[128,1,384]{2,1,0:T(1,128)S(1)} async-done(((f32[128,1,384]{2,1,0:T(1,128)}), f32[128,1,384]{2,1,0:T(1,128)S(1)}, u32[]{:S(2)}, u32[]{:S(2)}) %all-to-all-start) | async-done | bytes 196640 | tf_op jit(solution)/shard_map/all_to_all | solution.py:431
  24.8 0.0 collective-permute-done.hx_low_ref
  24.8 0.0 collective-permute-done.1.hx_high_ref
  24.8 0.0 collective-permute-done.2.hy_low_ref
  24.8 0.0 collective-permute-done.3.hy_high_ref
  24.9 4.9 %advance.1 = (f32[3,16,16,1024]{3,2,1,0:T(8,128)}, f32[3,16,1024]{2,1,0:T(8,128)S(1)}, f32[3,16,1024]{2,1,0:T(8,128)S(1)}, f32[3,16,1,1024]{3,2,1,0:T(1,128)S(1)...) custom-call(s32[2]{0:T(128)S(1)} %pad_add_fusion.at_ref, ...), custom_call_target="tpu_custom_call" | custom-call | tf_op jit(solution)/shard_map/advance/pallas_call | solution.py:455
  29.7 1.1 %collective-permute-start.4 = (f32[3,16,1024]{2,1,0:T(8,128)S(1)}, f32[3,16,1024]{2,1,0:T(8,128)S(1)}, u32[]{:S(2)}, u32[]{:S(2)}) collective-permute-start(f32[3,16,1024]{2,1,0:T(8,128)S(1)} %get-tuple-element.27), channel_id=1, source_target_pairs={{0,4},{4,8},{8,12},{12,16},{16,20},{20,24},{24,28},{28,32},{32,36}... | collective-permute-start | bytes 589832 | tf_op jit(solution)/shard_map/ppermute | solution.py:390
  30.8 1.7 %collective-permute-start.5 = (f32[3,16,1024]{2,1,0:T(8,128)S(1)}, f32[3,16,1024]{2,1,0:T(8,128)S(1)}, u32[]{:S(2)}, u32[]{:S(2)}) collective-permute-start(f32[3,16,1024]{2,1,0:T(8,128)S(1)} %get-tuple-element.28), channel_id=1, source_target_pairs={{0,124},{4,0},{8,4},{12,8},{16,12},{20,16},{24,20},{28,24},{32,28}... | collective-permute-start | bytes 589832 | tf_op jit(solution)/shard_map/ppermute | solution.py:391
  32.5 1.2 %collective-permute-start.6 = (f32[3,16,1,1024]{3,2,1,0:T(1,128)S(1)}, f32[3,16,1,1024]{3,2,1,0:T(1,128)S(1)}, u32[]{:S(2)}, u32[]{:S(2)}) collective-permute-start(f32[3,16,1,1024]{3,2,1,0:T(1,128)S(1)} %get-tuple-element.29), channel_id=1, source_target_pairs={{0,1},{1,2},{2,3},{3,0},{4,5},{5,6},{6,7},{7,4},{8,9},{9,10},{10,1... | collective-permute-start | bytes 589832 | tf_op jit(solution)/shard_map/ppermute | solution.py:392
  33.7 1.6 %collective-permute-start.7 = (f32[3,16,1,1024]{3,2,1,0:T(1,128)S(1)}, f32[3,16,1,1024]{3,2,1,0:T(1,128)S(1)}, u32[]{:S(2)}, u32[]{:S(2)}) collective-permute-start(f32[3,16,1,1024]{3,2,1,0:T(1,128)S(1)} %get-tuple-element.30), channel_id=1, source_target_pairs={{0,3},{1,0},{2,1},{3,2},{4,7},{5,4},{6,5},{7,6},{8,11},{9,8},{10,9... | collective-permute-start | bytes 589832 | tf_op jit(solution)/shard_map/ppermute | solution.py:393
  35.3 8.8 %all-to-all-start.1 = ((f32[128,1,384]{2,1,0:T(1,128)}), f32[128,1,384]{2,1,0:T(1,128)S(1)}, u32[]{:S(2)}, u32[]{:S(2)}) async-start(f32[128,1,384]{2,1,0:T(1,128)} %get-tuple-element.31), calls=%async_computation.1 | async-start | bytes 393216 | tf_op jit(solution)/shard_map/all_to_all | solution.py:473
  44.1 0.0 collective-permute-done.4.x_low_ref
  44.1 0.0 collective-permute-done.5.x_high_ref
  44.1 0.0 collective-permute-done.6.y_low_ref
  44.1 0.0 collective-permute-done.7.y_high_ref
  44.1 4.8 %finish.1 = f32[3,16,16,1024]{3,2,1,0:T(8,128)} custom-call(s32[2]{0:T(128)S(1)} %pad_add_fusion.at_ref, s32[64]{0:T(128)S(1)} %get-tuple-element.18.info_ref, f32[4,8,256]{2,1,0:T(8,128)S(1)} %get-tuple-element.25.force_ref, f32[3,16,16,1024]{3,2,1,0:T(8,128)} %get-tuple-element.26.field_ref, f32[3,16,1024]{2,1,0:T(8,128)S(1)} %collective-permute-done.4.x_low_ref, ...), custom_call_target="tpu_custom_call" | custom-call | tf_op jit(solution)/shard_map/finish/pallas_call | solution.py:475
  48.9 5.9 %all-to-all-done.1 = f32[128,1,384]{2,1,0:T(1,128)S(1)} async-done(((f32[128,1,384]{2,1,0:T(1,128)}), f32[128,1,384]{2,1,0:T(1,128)S(1)}, u32[]{:S(2)}, u32[]{:S(2)}) %all-to-all-start.1) | async-done | bytes 196640 | tf_op jit(solution)/shard_map/all_to_all | solution.py:473
  54.9 0.8 %reduce_sum.9 = f32[384]{0:T(512)} reduce(f32[128,1,384]{2,1,0:T(1,128)S(1)} %all-to-all-done.1, f32[]{:T(128)} %constant.10.clone.1), dimensions={0,1}, to_apply=%region_0.0 | reduce | flops 48768 | bytes 198148 | tf_op jit(solution)/shard_map/reduce_sum | solution.py:490
Async XLA Ops:
  0.6 18.2 %copy-start.1 = (s32[96]{0:T(128)S(1)}, s32[96]{0:T(128)}, u32[]{:S(2)}) copy-start(s32[96]{0:T(128)} %owner_ref.1) | copy-start | bytes 1156
  0.6 18.1 %copy-start = (s32[96,16]{0,1:T(8,128)S(1)}, s32[96,16]{0,1:T(8,128)}, u32[]{:S(2)}) copy-start(s32[96,16]{0,1:T(8,128)} %param.12) | copy-start | bytes 18436
  2.7 22.1 %all-to-all-start = ((f32[128,1,384]{2,1,0:T(1,128)}), f32[128,1,384]{2,1,0:T(1,128)S(1)}, u32[]{:S(2)}, u32[]{:S(2)}) async-start(f32[128,1,384]{2,1,0:T(1,128)} %get-tuple-element.20), calls=%async_computation | async-start | bytes 393216 | tf_op jit(solution)/shard_map/all_to_all | solution.py:431
  14.2 10.6 %collective-permute-start = (f32[3,16,1024]{2,1,0:T(8,128)S(1)}, f32[3,16,1024]{2,1,0:T(8,128)S(1)}, u32[]{:S(2)}, u32[]{:S(2)}) collective-permute-start(f32[3,16,1024]{2,1,0:T(8,128)S(1)} %get-tuple-element.21), channel_id=1, source_target_pairs={{0,4},{4,8},{8,12},{12,16},{16,20},{20,24},{24,28},{28,32},{32,36}... | collective-permute-start | bytes 589832 | tf_op jit(solution)/shard_map/ppermute | solution.py:390
  16.0 8.8 %collective-permute-start.1 = (f32[3,16,1024]{2,1,0:T(8,128)S(1)}, f32[3,16,1024]{2,1,0:T(8,128)S(1)}, u32[]{:S(2)}, u32[]{:S(2)}) collective-permute-start(f32[3,16,1024]{2,1,0:T(8,128)S(1)} %get-tuple-element.22), channel_id=1, source_target_pairs={{0,124},{4,0},{8,4},{12,8},{16,12},{20,16},{24,20},{28,24},{32,28}... | collective-permute-start | bytes 589832 | tf_op jit(solution)/shard_map/ppermute | solution.py:391
  16.0 8.8 %collective-permute-start.2 = (f32[3,16,1,1024]{3,2,1,0:T(1,128)S(1)}, f32[3,16,1,1024]{3,2,1,0:T(1,128)S(1)}, u32[]{:S(2)}, u32[]{:S(2)}) collective-permute-start(f32[3,16,1,1024]{3,2,1,0:T(1,128)S(1)} %get-tuple-element.23), channel_id=1, source_target_pairs={{0,1},{1,2},{2,3},{3,0},{4,5},{5,6},{6,7},{7,4},{8,9},{9,10},{10,1... | collective-permute-start | bytes 589832 | tf_op jit(solution)/shard_map/ppermute | solution.py:392
  17.2 7.6 %collective-permute-start.3 = (f32[3,16,1,1024]{3,2,1,0:T(1,128)S(1)}, f32[3,16,1,1024]{3,2,1,0:T(1,128)S(1)}, u32[]{:S(2)}, u32[]{:S(2)}) collective-permute-start(f32[3,16,1,1024]{3,2,1,0:T(1,128)S(1)} %get-tuple-element.24), channel_id=1, source_target_pairs={{0,3},{1,0},{2,1},{3,2},{4,7},{5,4},{6,5},{7,6},{8,11},{9,8},{10,9... | collective-permute-start | bytes 589832 | tf_op jit(solution)/shard_map/ppermute | solution.py:393
  29.7 14.4 %collective-permute-start.4 = (f32[3,16,1024]{2,1,0:T(8,128)S(1)}, f32[3,16,1024]{2,1,0:T(8,128)S(1)}, u32[]{:S(2)}, u32[]{:S(2)}) collective-permute-start(f32[3,16,1024]{2,1,0:T(8,128)S(1)} %get-tuple-element.27), channel_id=1, source_target_pairs={{0,4},{4,8},{8,12},{12,16},{16,20},{20,24},{24,28},{28,32},{32,36}... | collective-permute-start | bytes 589832 | tf_op jit(solution)/shard_map/ppermute | solution.py:390
  30.8 13.3 %collective-permute-start.5 = (f32[3,16,1024]{2,1,0:T(8,128)S(1)}, f32[3,16,1024]{2,1,0:T(8,128)S(1)}, u32[]{:S(2)}, u32[]{:S(2)}) collective-permute-start(f32[3,16,1024]{2,1,0:T(8,128)S(1)} %get-tuple-element.28), channel_id=1, source_target_pairs={{0,124},{4,0},{8,4},{12,8},{16,12},{20,16},{24,20},{28,24},{32,28}... | collective-permute-start | bytes 589832 | tf_op jit(solution)/shard_map/ppermute | solution.py:391
  32.5 11.6 %collective-permute-start.6 = (f32[3,16,1,1024]{3,2,1,0:T(1,128)S(1)}, f32[3,16,1,1024]{3,2,1,0:T(1,128)S(1)}, u32[]{:S(2)}, u32[]{:S(2)}) collective-permute-start(f32[3,16,1,1024]{3,2,1,0:T(1,128)S(1)} %get-tuple-element.29), channel_id=1, source_target_pairs={{0,1},{1,2},{2,3},{3,0},{4,5},{5,6},{6,7},{7,4},{8,9},{9,10},{10,1... | collective-permute-start | bytes 589832 | tf_op jit(solution)/shard_map/ppermute | solution.py:392
  33.7 10.4 %collective-permute-start.7 = (f32[3,16,1,1024]{3,2,1,0:T(1,128)S(1)}, f32[3,16,1,1024]{3,2,1,0:T(1,128)S(1)}, u32[]{:S(2)}, u32[]{:S(2)}) collective-permute-start(f32[3,16,1,1024]{3,2,1,0:T(1,128)S(1)} %get-tuple-element.30), channel_id=1, source_target_pairs={{0,3},{1,0},{2,1},{3,2},{4,7},{5,4},{6,5},{7,6},{8,11},{9,8},{10,9... | collective-permute-start | bytes 589832 | tf_op jit(solution)/shard_map/ppermute | solution.py:393
  35.3 19.6 %all-to-all-start.1 = ((f32[128,1,384]{2,1,0:T(1,128)}), f32[128,1,384]{2,1,0:T(1,128)S(1)}, u32[]{:S(2)}, u32[]{:S(2)}) async-start(f32[128,1,384]{2,1,0:T(1,128)} %get-tuple-element.31), calls=%async_computation.1 | async-start | bytes 393216 | tf_op jit(solution)/shard_map/all_to_all | solution.py:473
